TPU v7x, 256 devices: a whole 4x4x8 slice. The times are simulated.
256 devices in a mesh: dp: 4 (over z_hi), mx: 8 (over z_lo, y), my: 8 (over x, core).
Axes of the slice: x: 4, y: 4, z: 8 (z_hi: 4, z_lo: 2; z = z_hi * 2 + z_lo), core: 2. Of those that a mesh axis runs over, the one named last changes fastest.
Arguments:
- inputs: bfloat16 [768, 4096], P(('dp', 'mx', 'my')), may hold values from -6 to 6
- weight_means: bfloat16 [3, 14336, 4096], P(None, ('mx', 'my'), 'dp'), may hold values from -6 to 6
- weight_sigmas: bfloat16 [3, 14336, 4096], P(None, ('mx', 'my'), 'dp'), may hold values from 0.099609375 to 1
- weight_noise: bfloat16 [3, 14336, 4096], P(None, ('mx', 'my'), 'dp'), may hold values from -6 to 6
- input_signs: int32 [768, 4096], P(('dp', 'mx', 'my')), may hold values 0 or 1
- output_signs: int32 [2, 14336, 768], P(None, ('mx', 'my'), 'dp'), may hold values 0 or 1
- hidden_signs: int32 [14336, 768], P(('mx', 'my'), 'dp'), may hold values 0 or 1
- result_signs: int32 [768, 4096], P(('dp', 'mx', 'my')), may hold values 0 or 1
- cotangent: bfloat16 [768, 4096], P(('dp', 'mx', 'my')), may hold values from -6 to 6
Outputs:
- result: bfloat16 [768, 4096], P(('dp', 'mx', 'my'))
- input_grad: bfloat16 [768, 4096], P(('dp', 'mx', 'my'))
- mean_grad: bfloat16 [3, 14336, 4096], P(None, ('mx', 'my'), 'dp')
- sigma_grad: bfloat16 [3, 14336, 4096], P(None, ('mx', 'my'), 'dp')
All inputs are finite; a program needn't handle non-finite values. No bound on the sum of `input_signs` or of `output_signs` or of `hidden_signs` or of `result_signs` on one device may be relied on, other than what follows from the above.
Results may differ from a plain program's by a relative error of at most 0.02.
Values may be sent and summed in bfloat16 or wider, within the bound.
No kernel may reach another device: no remote copies, remote signals or barrier semaphores. Data moves between devices by JAX's collectives and lax.ppermute only.
A program may use at most 128 MiB of HBM per device.

v0:
```python
import jax
import jax.numpy as jnp
from jax import lax
from jax.experimental import pallas as pl
from jax.experimental.pallas import tpu as pltpu
from jax.sharding import Mesh, PartitionSpec as P


D = 4096
FF = 14336
SCALE_IN = D ** (-0.5)
SCALE_OUT = FF ** (-0.5)
F = 224
W = 1024
T = 192
G = 4
PK = 336
CHIP = ("zl", "y", "x")
ROWS = T * 8
SWAP = [(0, 1), (1, 0)]
BF = jnp.bfloat16
F32 = jnp.float32


def a2a(x, axes):
    return lax.all_to_all(x, axes, split_axis=0, concat_axis=0, tiled=True)


def shift(x, axis, by):
    return lax.ppermute(x, axis, [(i, (i + by) % 4) for i in range(4)])


def ring(block, axis):
    half = block.shape[0] // 2
    below, above = shift(block, axis, 1), shift(block, axis, -1)
    return below, above, shift(below[:half], axis, 1), shift(above[half:], axis, -1)


def pack(v):
    rest = jnp.concatenate([v[: F // 2, 128:T], v[F // 2 :, 128:T]], axis=1)
    return jnp.concatenate([v[:, :128], rest], axis=0)


def unpack(v):
    rest = v[F:]
    return jnp.concatenate([v[:F], jnp.concatenate([rest[:, :64], rest[:, 64:]], axis=0)], axis=1)


def nt(a, b):
    return lax.dot_general(a, b, (((1,), (1,)), ((), ())), preferred_element_type=F32)


def tn(a, b):
    return lax.dot_general(a, b, (((0,), (0,)), ((), ())), preferred_element_type=F32)


def nn(a, b):
    return lax.dot_general(a, b, (((1,), (0,)), ((), ())), preferred_element_type=F32)


ON_CHIP = pl.BlockSpec(memory_space=pltpu.VMEM)
SCALARS = pl.BlockSpec(memory_space=pltpu.SMEM)


def on_chip_call(body, args, out, scratch=(), mib=16, flops=0):
    moved = sum(a.size for a in args[1:]) * 2
    return pl.pallas_call(
        body,
        in_specs=[SCALARS] + [ON_CHIP] * (len(args) - 1),
        out_specs=[ON_CHIP] * len(out),
        out_shape=[jax.ShapeDtypeStruct(o, BF) for o in out],
        scratch_shapes=list(scratch),
        compiler_params=pltpu.CompilerParams(vmem_limit_bytes=mib * 1024 * 1024),
        cost_estimate=pl.CostEstimate(flops=flops, bytes_accessed=moved, transcendentals=0),
    )(*args)


def as_sign(values):
    return (2 * values - 1).astype(F32)


def prepare_body(pos, x_ref, a_ref, t_ref, r_ref, cols_ref, rows):
    for k, v in enumerate(
        (x_ref[...].astype(F32), as_sign(a_ref[...]), t_ref[...].astype(F32), as_sign(r_ref[...]))
    ):
        for d in range(G):
            rel = (d - pos[0]) & 3
            for j in range(8):
                at = (8 * d + j) * 128
                rows[rel, k, pl.ds(j, 3, stride=8)] = v[:, at : at + 128]
    cols_ref[...] = rows[...].astype(BF)


def prepare(*args):
    return on_chip_call(
        prepare_body, args, [(G, 4, 24, 128)], scratch=[pltpu.VMEM((G, 4, 24, 128), F32)]
    )[0]


def signs_body(_, s_ref, h_ref, o_ref):
    for k in range(3):
        v = s_ref[k] if k < 2 else h_ref[...]
        o_ref[k * PK : (k + 1) * PK] = pack(as_sign(v)).astype(BF)


def packed_signs(*args):
    return on_chip_call(signs_body, args, [(3 * PK, 128)])[0]


def finish_body(pos, p0, p1, p2, p3, res_ref, inp_ref, rows):
    for j, ref in enumerate((p0, p1, p2, p3)):
        rows[(pos[0] + j) & 3] = ref[...].astype(F32)
    for k, o_ref in enumerate((res_ref, inp_ref)):
        for d in range(G):
            for j in range(8):
                at = (8 * d + j) * 128
                o_ref[:, at : at + 128] = rows[d, pl.ds(24 * k + j, 3, stride=8)].astype(BF)


def finish(*args):
    return on_chip_call(
        finish_body, args, [(3, D), (3, D)], scratch=[pltpu.VMEM((G, 48, 128), F32)]
    )


def perturb_body(s_ref, n_ref, o_ref):
    o_ref[...] = (s_ref[...].astype(F32) * n_ref[...].astype(F32)).astype(BF)


def perturbation(sigmas, noise):
    spec = pl.BlockSpec((1, F, W), lambda i: (i, 0, 0))
    return pl.pallas_call(
        perturb_body,
        grid=(3,),
        in_specs=[spec, spec],
        out_specs=spec,
        out_shape=jax.ShapeDtypeStruct((3, F, W), BF),
        compiler_params=pltpu.CompilerParams(vmem_limit_bytes=8 * 1024 * 1024),
        name="perturbation",
    )(sigmas, noise)


def assemble_body(pos, *refs):
    pieces, (plain_ref, sign_ref, both) = refs[:16], refs[16:]
    zl, y, x, c = pos[1], pos[2], pos[3], pos[4]

    def one_group(g, carry):
        for src in range(2):
            for k in range(2):
                col = c if k == 0 else 1 - c
                for outer in range(4):
                    ref = pieces[8 * src + 4 * k + outer]

                    def place(i, carry):
                        dy, dx = (outer, i) if src == 0 else (i, outer)
                        my = 2 * ((x + dx) & 3) + col
                        for z in range(2):
                            mx = (zl if z == 0 else 1 - zl) * 4 + ((y + dy) & 3)
                            at = pl.ds(pl.multiple_of((mx * 8 + my) * 24, 8), 24)
                            for a in range(2):
                                both[a, at] = ref[i, z, a, g].astype(F32)
                        return carry

                    lax.fori_loop(0, 4, place, 0)
            for a, o_ref in ((0, plain_ref), (1, sign_ref)):
                for j in range(8):
                    o_ref[src, g, :, j * 128 : (j + 1) * 128] = both[a, pl.ds(j, T, stride=8)].astype(BF)
        return carry

    lax.fori_loop(0, G, one_group, 0)


def assemble(pos, pieces):
    return on_chip_call(
        assemble_body, [pos, *pieces], [(2, G, T, W)] * 2, scratch=[pltpu.VMEM((2, ROWS, 128), F32)]
    )


def gather(both, inner, outer):
    line = jnp.stack([both, shift(both, inner, -1), shift(both, inner, 2), shift(both, inner, 1)])
    below = shift(line, outer, 1)
    above = shift(line, outer, -1)
    own = [line, above, shift(below, outer, 1), below]
    return own + [lax.ppermute(p, "c", SWAP) for p in own]


def scale_of(k):
    return jnp.where(k == 2, jnp.float32(SCALE_OUT), jnp.float32(SCALE_IN))


def packed_rows(k):
    return pl.ds(pl.multiple_of(k * PK, 16), PK)


def project_body(rels, pos, x_ref, a_ref, m_ref, p_ref, *refs):
    s_refs, o_ref = refs[:-1], refs[-1]
    for i, rel in enumerate(rels):

        def one(k, carry):
            plain = x_ref[k >> 1, rel]
            flip = plain * a_ref[k >> 1, rel]
            mean = pack(nt(m_ref[k], plain))
            pert = pack(nt(p_ref[k], flip))
            sign = s_refs[i][packed_rows(k)].astype(F32)
            scale = scale_of(k)
            o_ref[i, packed_rows(k)] = (scale * mean + scale * pert * sign).astype(BF)
            return carry

        lax.fori_loop(0, 3, one, 0)


def project(pos, acts, means, perturb, signs, rels):
    return on_chip_call(
        lambda *refs: project_body(rels, *refs),
        [pos, *acts, means, perturb, *(signs[rel] for rel in rels)],
        [(len(rels), 3 * PK, 128)],
        flops=len(rels) * 12 * F * W * T,
    )[0]


def pointwise_body(a_ref, b_ref, c_ref, o_ref):
    def total(k):
        at = slice(k * PK, (k + 1) * PK)
        return a_ref[at].astype(F32) + b_ref[at].astype(F32) + c_ref[at].astype(F32)

    gate, up, dh = total(0), total(1), total(2)
    sig = jax.nn.sigmoid(gate)
    o_ref[0:PK] = (dh * up * sig * (1.0 + gate * (1.0 - sig))).astype(BF)
    o_ref[PK : 2 * PK] = (dh * gate * sig).astype(BF)
    o_ref[2 * PK :] = (gate * sig * up).astype(BF)


def pointwise(pos, a, b, c):
    return on_chip_call(lambda _, *refs: pointwise_body(*refs), [pos, a, b, c], [(3 * PK, 128)])[0]


def back_body(rels, pos, a_ref, m_ref, p_ref, *refs):
    n = len(rels)
    h_refs, s_refs, o_ref, rows = refs[:n], refs[n : 2 * n], refs[2 * n], refs[2 * n + 1]
    c = pos[4]
    for i, rel in enumerate(rels):

        def one(k, carry):
            h = h_refs[i][packed_rows(k)]
            mean = tn(unpack(h), m_ref[k])
            pert = tn(unpack(h * s_refs[i][packed_rows(k)]), p_ref[k])
            scale = scale_of(k)
            v = scale * mean + scale * pert * a_ref[k >> 1, rel].astype(F32)
            for q in range(8):
                at = pl.ds(q, T, stride=8)
                before = jnp.where(k == 1, rows[k >> 1, at], 0.0)
                rows[k >> 1, at] = before + v[:, q * 128 : (q + 1) * 128]
            return carry

        lax.fori_loop(0, 3, one, 0)

        def place(q, carry):
            for j in range(2):
                for col in range(2):
                    at = pl.multiple_of(q * 48 + col * 24, 8)
                    half = c if col == 0 else 1 - c
                    o_ref[half, q, i, j] = rows[1 - j, pl.ds(at, 24)].astype(BF)
            return carry

        lax.fori_loop(0, 32, place, 0)


def back(pos, h, signs, a, means, perturb, rels):
    return on_chip_call(
        lambda *refs: back_body(rels, *refs),
        [pos, a, means, perturb, *h, *(signs[rel] for rel in rels)],
        [(2, 32, len(rels), 2, 24, 128)],
        scratch=[pltpu.VMEM((2, ROWS, 128), F32)],
        flops=len(rels) * 12 * F * W * T,
    )[0]


def grads_body(*refs):
    hs, signs = refs[:4], refs[4:8]
    x_ref, a_ref, n_ref, mo_ref, so_ref, lhs, sums = refs[8:]

    @pl.when(pl.program_id(0) == 0)
    def _():
        def one(k, carry):
            for rel in range(G):
                v = hs[rel][packed_rows(k)]
                lhs[rel, 2 * k] = unpack(v)
                lhs[rel, 2 * k + 1] = unpack(v * signs[rel][packed_rows(k)])
            return carry

        lax.fori_loop(0, 3, one, 0)

    sums[...] = jnp.zeros(sums.shape, F32)

    def one_term(at, carry):
        rel, k = at & 3, at >> 2
        plain = x_ref[k >> 1, rel]
        for j, rhs in enumerate((plain, plain * a_ref[k >> 1, rel])):
            term = scale_of(k) * nn(lhs[rel, 2 * k + j], rhs)
            sums[2 * k + j] += term.astype(BF).astype(F32)
        return carry

    lax.fori_loop(0, 3 * G, one_term, 0)
    for k in range(3):
        mo_ref[k] = sums[2 * k].astype(BF)
        so_ref[k] = (sums[2 * k + 1] * n_ref[k].astype(F32)).astype(BF)


def grads(h, signs, acts, noise):
    w = pl.BlockSpec((3, F, 256), lambda i: (0, 0, i))
    group = pl.BlockSpec((2, G, T, 256), lambda i: (0, 0, 0, i))
    out = jax.ShapeDtypeStruct((3, F, W), BF)
    return pl.pallas_call(
        grads_body,
        grid=(4,),
        in_specs=[ON_CHIP] * 8 + [group] * 2 + [w],
        out_specs=[w, w],
        scratch_shapes=[pltpu.VMEM((G, 6, F, T), BF), pltpu.VMEM((6, F, 256), F32)],
        out_shape=[out, out],
        compiler_params=pltpu.CompilerParams(vmem_limit_bytes=28 * 1024 * 1024),
        cost_estimate=pl.CostEstimate(
            flops=48 * F * W * T, bytes_accessed=8 * G * T * W + 18 * F * W, transcendentals=0
        ),
        name="grads",
    )(*h, *signs, *acts, noise)


def merged(out):
    return (out[0].astype(F32) + lax.ppermute(out[1], "c", SWAP).astype(F32)).astype(BF)


def over_dp(rel):
    return [rel[0]] + [shift(rel[4 - j], "dp", 4 - j) for j in range(1, 4)]


def on_device(
    inputs,
    weight_means,
    weight_sigmas,
    weight_noise,
    input_signs,
    output_signs,
    hidden_signs,
    result_signs,
    cotangent,
):
    place = [lax.axis_index(name) for name in ("dp", "zl", "y", "x", "c")]
    pos = jnp.stack(place).astype(jnp.int32)
    cols = over_dp(prepare(pos, inputs, input_signs, cotangent, result_signs))
    perturb = perturbation(weight_sigmas, weight_noise)
    cols = jnp.stack(cols, axis=1)
    cols = jnp.stack([cols, lax.ppermute(cols, "zl", SWAP)])
    signs = packed_signs(pos, output_signs, hidden_signs)
    below, above = shift(signs, "dp", 1), shift(signs, "dp", -1)
    signs = [signs, above, shift(below, "dp", 1), below]
    xs = gather(cols[:, :2], "x", "y")
    cs = gather(cols[:, 2:], "y", "x")
    acts = assemble(pos, xs + cs)

    half = 3 * PK // 2
    far = project(pos, acts, weight_means, perturb, signs, (2,))[0]
    from_below = shift(far[:half], "dp", 1)
    from_above = shift(far[half:], "dp", -1)
    near = project(pos, acts, weight_means, perturb, signs, (1, 3))

    def plus(u, v):
        return (u.astype(F32) + v.astype(F32)).astype(BF)

    up = jnp.concatenate([plus(near[0, :half], from_below), near[0, half:]])
    down = jnp.concatenate([near[1, :half], plus(near[1, half:], from_above)])
    up, down = shift(up, "dp", 1), shift(down, "dp", -1)
    own = project(pos, acts, weight_means, perturb, signs, (0,))[0]
    h = pointwise(pos, own, up, down)

    below, above, first, second = ring(h, "dp")
    h = [h, above, jnp.concatenate([first, second]), below]
    outs = []
    for rels in ((0,), (1, 3), (2,)):
        outs.append(merged(back(pos, [h[j] for j in rels], signs, acts[1], weight_means, perturb, rels)))
    got = jnp.concatenate(outs, axis=1).reshape(32, 192, 128)
    got = a2a(got, CHIP)
    mean_grad, sigma_grad = grads(h, signs, acts, weight_noise)
    got = jnp.sum(got.astype(F32), axis=0).astype(BF)
    got = over_dp([got[:48], got[48:96], got[144:], got[96:144]])
    result, input_grad = finish(pos, *got)
    return result, input_grad, mean_grad, sigma_grad


def solution(mesh):
    fine = Mesh(mesh.devices.reshape(4, 2, 4, 4, 2), ("dp", "zl", "y", "x", "c"))
    tok = P(("dp", "zl", "y", "x", "c"), None)
    ff = ("zl", "y", "x", "c")
    wide = P(None, ff, "dp")

    return jax.shard_map(
        on_device,
        mesh=fine,
        in_specs=(tok, wide, wide, wide, tok, wide, P(ff, "dp"), tok, tok),
        out_specs=(tok, tok, wide, wide),
        check_vma=False,
    )
```

profile of v0, /device:TPU:8, one launch (start us, length us, event | category | flops | bytes accessed | tf_op | source)
XLA Modules:
  0.0 199.9 jit_solution(4200239945088032853)
XLA Ops:
  0.7 0.8 copy-done.20
  1.6 0.8 copy-done.21
  2.4 0.8 copy-done.22
  3.2 0.8 copy-done.23
  4.6 3.3 %collective-permute-start.2 = (bf16[4,24,128]{2,1,0:T(8,128)(2,1)S(1)}, bf16[4,24,128]{2,1,0:T(8,128)(2,1)S(1)}, u32[]{:S(2)}, u32[]{:S(2)}) collective-permute-start(bf16[4,24,128]{2,1,0:T(8,128)(2,1)S(1)} %get-tuple-element.27), channel_id=1, source_target_pairs={{0,64},{64,128},{128,192},{192,0},{1,65},{65,129},{129,193},{193,1... | collective-permute-start | bytes 73736 | tf_op jit(solution)/shard_map/ppermute | solution.py:30
  7.9 3.1 %collective-permute-start = (bf16[4,24,128]{2,1,0:T(8,128)(2,1)S(1)}, bf16[4,24,128]{2,1,0:T(8,128)(2,1)S(1)}, u32[]{:S(2)}, u32[]{:S(2)}) collective-permute-start(bf16[4,24,128]{2,1,0:T(8,128)(2,1)S(1)} %get-tuple-element.29), channel_id=1, source_target_pairs={{0,192},{64,0},{128,64},{192,128},{1,193},{65,1},{129,65},{193,129... | collective-permute-start | bytes 73736 | tf_op jit(solution)/shard_map/ppermute | solution.py:30
  11.0 4.9 %collective-permute-start.1 = (bf16[4,24,128]{2,1,0:T(8,128)(2,1)S(1)}, bf16[4,24,128]{2,1,0:T(8,128)(2,1)S(1)}, u32[]{:S(2)}, u32[]{:S(2)}) collective-permute-start(bf16[4,24,128]{2,1,0:T(8,128)(2,1)S(1)} %get-tuple-element.28), channel_id=1, source_target_pairs={{0,128},{64,192},{128,0},{192,64},{1,129},{65,193},{129,1},{193,65... | collective-permute-start | bytes 73736 | tf_op jit(solution)/shard_map/ppermute | solution.py:30
  16.0 2.8 %collective-permute-done.1 = bf16[4,24,128]{2,1,0:T(8,128)(2,1)S(1)} collective-permute-done((bf16[4,24,128]{2,1,0:T(8,128)(2,1)S(1)}, bf16[4,24,128]{2,1,0:T(8,128)(2,1)S(1)}, u32[]{:S(2)}, u32[]{:S(2)}) %collective-permute-start.1) | collective-permute-done | bytes 24608 | tf_op jit(solution)/shard_map/ppermute | solution.py:30
  18.8 1.1 collective-permute-start.3
  19.9 3.6 %collective-permute-done.3 = bf16[4,4,24,128]{3,2,1,0:T(8,128)(2,1)S(1)} collective-permute-done((bf16[4,4,24,128]{3,2,1,0:T(8,128)(2,1)S(1)}, bf16[4,4,24,128]{3,2,1,0:T(8,128)(2,1)S(1)}, u32[]{:S(2)}, u32[]{:S(2)}) %collective-permute-start.3) | collective-permute-done | bytes 98336 | tf_op jit(solution)/shard_map/ppermute | solution.py:352
  24.0 2.6 %collective-permute-start.15 = (bf16[2,2,4,24,128]{4,3,2,1,0:T(8,128)(2,1)S(1)}, bf16[2,2,4,24,128]{4,3,2,1,0:T(8,128)(2,1)S(1)}, u32[]{:S(2)}, u32[]{:S(2)}) collective-permute-start(bf16[2,2,4,24,128]{4,3,2,1,0:T(8,128)(2,1)S(1)} %get-tuple-element.22), channel_id=1, source_target_pairs={{0,16},{8,24},{16,0},{24,8},{1,17},{9,25},{17,1},{25,9},{2,18},{10... | collective-permute-start | bytes 294920 | tf_op jit(solution)/shard_map/ppermute | solution.py:30
  26.6 1.9 collective-permute-start.16
  28.5 1.2 copy.13.s_ref
  29.9 0.6 shard_map.122.refs_5_.refs_4_
  30.5 1.4 collective-permute-start.25
  32.0 2.8 %collective-permute-start.4 = (bf16[2,2,4,24,128]{4,3,2,1,0:T(8,128)(2,1)S(1)}, bf16[2,2,4,24,128]{4,3,2,1,0:T(8,128)(2,1)S(1)}, u32[]{:S(2)}, u32[]{:S(2)}) collective-permute-start(bf16[2,2,4,24,128]{4,3,2,1,0:T(8,128)(2,1)S(1)} %get-tuple-element.23), channel_id=1, source_target_pairs={{0,6},{2,0},{4,2},{6,4},{1,7},{3,1},{5,3},{7,5},{8,14},{10,8},{12,... | collective-permute-start | bytes 294920 | tf_op jit(solution)/shard_map/ppermute | solution.py:30
  34.7 0.8 collective-permute-start.5
  35.5 0.9 collective-permute-start.6
  36.5 1.9 collective-permute-start.18
  38.4 2.4 %collective-permute-start.17 = (bf16[4,2,2,4,24,128]{5,4,3,2,1,0:T(8,128)(2,1)S(1)}, bf16[4,2,2,4,24,128]{5,4,3,2,1,0:T(8,128)(2,1)S(1)}, u32[]{:S(2)}, u32[]{:S(2)}) collective-permute-start(bf16[4,2,2,4,24,128]{5,4,3,2,1,0:T(8,128)(2,1)S(1)} %pad_maximum_fusion.2.refs_8_), channel_id=1, source_target_pairs={{0,6},{2,0},{4,2},{6,4},{1,7},{3,1},{5,3},{7,5},{8,14},{10,8},{12,... | collective-permute-start | bytes 1179656 | tf_op jit(solution)/shard_map/ppermute | solution.py:30
  40.8 1.1 collective-permute-done.5
  41.9 1.2 collective-permute-done.6
  43.3 1.9 collective-permute-start.7
  45.3 2.0 %collective-permute-done.18.refs_11_ = bf16[4,2,2,4,24,128]{5,4,3,2,1,0:T(8,128)(2,1)S(1)} collective-permute-done((bf16[4,2,2,4,24,128]{5,4,3,2,1,0:T(8,128)(2,1)S(1)}, bf16[4,2,2,4,24,128]{5,4,3,2,1,0:T(8,128)(2,1)S(1)}, u32[]{:S(2)}, u32[]{:S(2)}) %collective-permute-start.18) | collective-permute-done | bytes 393248 | tf_op jit(solution)/shard_map/ppermute | solution.py:30
  47.9 5.6 %collective-permute-done.8.refs_3_ = bf16[4,2,2,4,24,128]{5,4,3,2,1,0:T(8,128)(2,1)S(1)} collective-permute-done((bf16[4,2,2,4,24,128]{5,4,3,2,1,0:T(8,128)(2,1)S(1)}, bf16[4,2,2,4,24,128]{5,4,3,2,1,0:T(8,128)(2,1)S(1)}, u32[]{:S(2)}, u32[]{:S(2)}) %collective-permute-start.8) | collective-permute-done | bytes 393248 | tf_op jit(solution)/shard_map/ppermute | solution.py:30
  54.4 5.7 %collective-permute-done.19.refs_10_ = bf16[4,2,2,4,24,128]{5,4,3,2,1,0:T(8,128)(2,1)S(1)} collective-permute-done((bf16[4,2,2,4,24,128]{5,4,3,2,1,0:T(8,128)(2,1)S(1)}, bf16[4,2,2,4,24,128]{5,4,3,2,1,0:T(8,128)(2,1)S(1)}, u32[]{:S(2)}, u32[]{:S(2)}) %collective-permute-start.19) | collective-permute-done | bytes 393248 | tf_op jit(solution)/shard_map/ppermute | solution.py:30
  60.6 2.5 %collective-permute-done.9.refs_2_ = bf16[4,2,2,4,24,128]{5,4,3,2,1,0:T(8,128)(2,1)S(1)} collective-permute-done((bf16[4,2,2,4,24,128]{5,4,3,2,1,0:T(8,128)(2,1)S(1)}, bf16[4,2,2,4,24,128]{5,4,3,2,1,0:T(8,128)(2,1)S(1)}, u32[]{:S(2)}, u32[]{:S(2)}) %collective-permute-start.9) | collective-permute-done | bytes 393248 | tf_op jit(solution)/shard_map/ppermute | solution.py:30
  63.0 4.4 %collective-permute-start.26 = (bf16[1008,128]{1,0:T(8,128)(2,1)S(1)}, bf16[1008,128]{1,0:T(8,128)(2,1)S(1)}, u32[]{:S(2)}, u32[]{:S(2)}) collective-permute-start(bf16[1008,128]{1,0:T(8,128)(2,1)S(1)} %collective-permute-done.25.refs_6_.refs_7_), channel_id=1, source_target_pairs={{0,64},{64,128},{128,192},{192,0},{1,65},{65,129},{129,193},{193,1... | collective-permute-start | bytes 774152 | tf_op jit(solution)/shard_map/ppermute | solution.py:30
  67.9 5.9 %shard_map.121 = (bf16[2,4,192,1024]{3,2,1,0:T(8,128)(2,1)S(1)}, bf16[2,4,192,1024]{3,2,1,0:T(8,128)(2,1)S(1)}) custom-call(s32[5]{0:T(128)S(1)} %stack.74.pos._.refs_0_, bf16[4,2,2,4,24,128]{5,4,3,2,1,0:T(8,128)(2,1)S(1)} %pad_maximum_fusion.1.refs_0_, bf16[4,2,2,4,24,128]{5,4,3,2,1,0:T(8,128)(2,1)S(1)} %collective-permute-done.7.refs_1_, ...), custom_call_target="tpu_custom_call" | custom-call | bytes 6291456 | tf_op jit(solution)/shard_map/pallas_call | solution.py:67
  73.8 4.7 %collective-permute-done.26.refs_5_.refs_6_ = bf16[1008,128]{1,0:T(8,128)(2,1)S(1)} collective-permute-done((bf16[1008,128]{1,0:T(8,128)(2,1)S(1)}, bf16[1008,128]{1,0:T(8,128)(2,1)S(1)}, u32[]{:S(2)}, u32[]{:S(2)}) %collective-permute-start.26) | collective-permute-done | bytes 258080 | tf_op jit(solution)/shard_map/ppermute | solution.py:30
  78.6 2.1 %shard_map.125 = bf16[1,1008,128]{2,1,0:T(8,128)(2,1)S(1)} custom-call(s32[5]{0:T(128)S(1)} %stack.74.pos._.refs_0_, bf16[2,4,192,1024]{3,2,1,0:T(8,128)(2,1)S(1)} %get-tuple-element.11.refs_1_.refs_8_, bf16[2,4,192,1024]{3,2,1,0:T(8,128)(2,1)S(1)} %get-tuple-element.10.refs_2_.refs_1_.refs_9_, bf16[3,224,1024]{2,1,0:T(8,128)(2,1)S(1)} %copy-done.2, ...), custom_call_target="tpu_custom_call" | custom-call | flops 528482304 | bytes 9302016 | tf_op jit(solution)/shard_map/pallas_call | solution.py:67
  80.7 3.5 %collective-permute-start.27 = (bf16[504,128]{1,0:T(8,128)(2,1)S(1)}, bf16[504,128]{1,0:T(8,128)(2,1)S(1)}, u32[]{:S(2)}, u32[]{:S(2)}) collective-permute-start(bf16[504,128]{1,0:T(8,128)(2,1)S(1)} %get-tuple-element.21), channel_id=1, source_target_pairs={{0,64},{64,128},{128,192},{192,0},{1,65},{65,129},{129,193},{193,1... | collective-permute-start | bytes 387080 | tf_op jit(solution)/shard_map/ppermute | solution.py:30
  84.2 0.7 collective-permute-start.29
  84.9 3.6 %shard_map.124 = bf16[2,1008,128]{2,1,0:T(8,128)(2,1)S(1)} custom-call(s32[5]{0:T(128)S(1)} %stack.74.pos._.refs_0_, bf16[2,4,192,1024]{3,2,1,0:T(8,128)(2,1)S(1)} %get-tuple-element.11.refs_1_.refs_8_, bf16[2,4,192,1024]{3,2,1,0:T(8,128)(2,1)S(1)} %get-tuple-element.10.refs_2_.refs_1_.refs_9_, bf16[3,224,1024]{2,1,0:T(8,128)(2,1)S(1)} %copy-done.2, ...), custom_call_target="tpu_custom_call" | custom-call | flops 1056964608 | bytes 9560064 | tf_op jit(solution)/shard_map/pallas_call | solution.py:67
  88.6 2.4 %collective-permute-done.27 = bf16[504,128]{1,0:T(8,128)(2,1)S(1)} collective-permute-done((bf16[504,128]{1,0:T(8,128)(2,1)S(1)}, bf16[504,128]{1,0:T(8,128)(2,1)S(1)}, u32[]{:S(2)}, u32[]{:S(2)}) %collective-permute-start.27) | collective-permute-done | bytes 129056 | tf_op jit(solution)/shard_map/ppermute | solution.py:30
  90.9 0.7 collective-permute-done.29
  91.8 2.1 %collective-permute-start.30 = (bf16[1008,128]{1,0:T(8,128)(2,1)S(1)}, bf16[1008,128]{1,0:T(8,128)(2,1)S(1)}, u32[]{:S(2)}, u32[]{:S(2)}) collective-permute-start(bf16[1008,128]{1,0:T(8,128)(2,1)S(1)} %pad_maximum_fusion.4), channel_id=1, source_target_pairs={{0,192},{64,0},{128,64},{192,128},{1,193},{65,1},{129,65},{193,129... | collective-permute-start | bytes 774152 | tf_op jit(solution)/shard_map/ppermute | solution.py:30
  93.9 1.2 collective-permute-start.28
  95.1 2.1 %shard_map.123 = bf16[1,1008,128]{2,1,0:T(8,128)(2,1)S(1)} custom-call(s32[5]{0:T(128)S(1)} %stack.74.pos._.refs_0_, bf16[2,4,192,1024]{3,2,1,0:T(8,128)(2,1)S(1)} %get-tuple-element.11.refs_1_.refs_8_, bf16[2,4,192,1024]{3,2,1,0:T(8,128)(2,1)S(1)} %get-tuple-element.10.refs_2_.refs_1_.refs_9_, bf16[3,224,1024]{2,1,0:T(8,128)(2,1)S(1)} %copy-done.2, ...), custom_call_target="tpu_custom_call" | custom-call | flops 528482304 | bytes 9302016 | tf_op jit(solution)/shard_map/pallas_call | solution.py:67
  97.2 8.7 %collective-permute-done.30.refs_2_ = bf16[1008,128]{1,0:T(8,128)(2,1)S(1)} collective-permute-done((bf16[1008,128]{1,0:T(8,128)(2,1)S(1)}, bf16[1008,128]{1,0:T(8,128)(2,1)S(1)}, u32[]{:S(2)}, u32[]{:S(2)}) %collective-permute-start.30) | collective-permute-done | bytes 258080 | tf_op jit(solution)/shard_map/ppermute | solution.py:30
  105.9 2.8 %collective-permute-done.28.refs_1_ = bf16[1008,128]{1,0:T(8,128)(2,1)S(1)} collective-permute-done((bf16[1008,128]{1,0:T(8,128)(2,1)S(1)}, bf16[1008,128]{1,0:T(8,128)(2,1)S(1)}, u32[]{:S(2)}, u32[]{:S(2)}) %collective-permute-start.28) | collective-permute-done | bytes 258080 | tf_op jit(solution)/shard_map/ppermute | solution.py:30
  108.7 0.7 shard_map.126.refs_4_.refs_0_
  109.5 4.1 %collective-permute-start.32 = (bf16[1008,128]{1,0:T(8,128)(2,1)S(1)}, bf16[1008,128]{1,0:T(8,128)(2,1)S(1)}, u32[]{:S(2)}, u32[]{:S(2)}) collective-permute-start(bf16[1008,128]{1,0:T(8,128)(2,1)S(1)} %shard_map.126.refs_4_.refs_0_), channel_id=1, source_target_pairs={{0,192},{64,0},{128,64},{192,128},{1,193},{65,1},{129,65},{193,129... | collective-permute-start | bytes 774152 | tf_op jit(solution)/shard_map/ppermute | solution.py:30
  113.7 2.6 %shard_map.127 = bf16[2,32,1,2,24,128]{5,4,3,2,1,0:T(8,128)(2,1)S(1)} custom-call(s32[5]{0:T(128)S(1)} %stack.74.pos._.refs_0_, bf16[2,4,192,1024]{3,2,1,0:T(8,128)(2,1)S(1)} %get-tuple-element.10.refs_2_.refs_1_.refs_9_, bf16[3,224,1024]{2,1,0:T(8,128)(2,1)S(1)} %copy-done.2, bf16[3,224,1024]{2,1,0:T(8,128)(2,1)S(1)} %perturbation.1.refs_4_.refs_3_, ...), custom_call_target="tpu_custom_call" | custom-call | flops 528482304 | bytes 6414336 | tf_op jit(solution)/shard_map/pallas_call | solution.py:67
  116.5 7.4 %collective-permute-done.33.refs_5_.refs_3_ = bf16[1008,128]{1,0:T(8,128)(2,1)S(1)} collective-permute-done((bf16[1008,128]{1,0:T(8,128)(2,1)S(1)}, bf16[1008,128]{1,0:T(8,128)(2,1)S(1)}, u32[]{:S(2)}, u32[]{:S(2)}) %collective-permute-start.33) | collective-permute-done | bytes 258080 | tf_op jit(solution)/shard_map/ppermute | solution.py:30
  124.0 4.2 %collective-permute-start.36 = (bf16[504,128]{1,0:T(8,128)(2,1)S(1)}, bf16[504,128]{1,0:T(8,128)(2,1)S(1)}, u32[]{:S(2)}, u32[]{:S(2)}) collective-permute-start(bf16[504,128]{1,0:T(8,128)(2,1)S(1)} %slice.121), channel_id=1, source_target_pairs={{0,192},{64,0},{128,64},{192,128},{1,193},{65,1},{129,65},{193,129... | collective-permute-start | bytes 387080 | tf_op jit(solution)/shard_map/ppermute | solution.py:30
  128.2 4.7 %shard_map.128 = bf16[2,32,2,2,24,128]{5,4,3,2,1,0:T(8,128)(2,1)S(1)} custom-call(s32[5]{0:T(128)S(1)} %stack.74.pos._.refs_0_, bf16[2,4,192,1024]{3,2,1,0:T(8,128)(2,1)S(1)} %get-tuple-element.10.refs_2_.refs_1_.refs_9_, bf16[3,224,1024]{2,1,0:T(8,128)(2,1)S(1)} %copy-done.2, bf16[3,224,1024]{2,1,0:T(8,128)(2,1)S(1)} %perturbation.1.refs_4_.refs_3_, ...), custom_call_target="tpu_custom_call" | custom-call | flops 1056964608 | bytes 6930432 | tf_op jit(solution)/shard_map/pallas_call | solution.py:67
  133.2 2.6 %shard_map.129 = bf16[2,32,1,2,24,128]{5,4,3,2,1,0:T(8,128)(2,1)S(1)} custom-call(s32[5]{0:T(128)S(1)} %stack.74.pos._.refs_0_, bf16[2,4,192,1024]{3,2,1,0:T(8,128)(2,1)S(1)} %get-tuple-element.10.refs_2_.refs_1_.refs_9_, bf16[3,224,1024]{2,1,0:T(8,128)(2,1)S(1)} %copy-done.2, bf16[3,224,1024]{2,1,0:T(8,128)(2,1)S(1)} %perturbation.1.refs_4_.refs_3_, ...), custom_call_target="tpu_custom_call" | custom-call | flops 528482304 | bytes 6414336 | tf_op jit(solution)/shard_map/pallas_call | solution.py:67
  136.5 1.2 collective-permute-done.37
  138.3 28.3 %all_to_all.5 = bf16[32,192,128]{2,1,0:T(8,128)(2,1)} all-to-all(bf16[32,192,128]{2,1,0:T(8,128)(2,1)S(1)} %bitcast.76), channel_id=1, replica_groups=mesh['dp'=4,'zl'=2,'y'=4,'x'=4,'c'=2] {'zl','y','x'}, dimensions={0} | all-to-all | bytes 3145728 | tf_op jit(solution)/shard_map/all_to_all | solution.py:26
  166.6 1.6 reduce_sum.12
  168.2 3.1 %collective-permute-start.38 = (bf16[48,128]{1,0:T(8,128)(2,1)S(1)}, bf16[48,128]{1,0:T(8,128)(2,1)S(1)}, u32[]{:S(2)}, u32[]{:S(2)}) collective-permute-start(bf16[48,128]{1,0:T(8,128)(2,1)S(1)} %get-tuple-element.32), channel_id=1, source_target_pairs={{0,192},{64,0},{128,64},{192,128},{1,193},{65,1},{129,65},{193,129... | collective-permute-start | bytes 36872 | tf_op jit(solution)/shard_map/ppermute | solution.py:30
  171.3 3.9 %collective-permute-start.39 = (bf16[48,128]{1,0:T(8,128)(2,1)S(1)}, bf16[48,128]{1,0:T(8,128)(2,1)S(1)}, u32[]{:S(2)}, u32[]{:S(2)}) collective-permute-start(bf16[48,128]{1,0:T(8,128)(2,1)S(1)} %get-tuple-element.31), channel_id=1, source_target_pairs={{0,128},{64,192},{128,0},{192,64},{1,129},{65,193},{129,1},{193,65... | collective-permute-start | bytes 36872 | tf_op jit(solution)/shard_map/ppermute | solution.py:30
  175.2 1.9 copy-done.1
  177.1 1.3 copy-done.4
  178.4 0.9 copy-done.6
  179.4 0.9 copy-done.8
  180.3 0.9 copy-done.10
  181.3 0.9 copy-done.12
  182.2 0.9 copy-done.14
  183.2 0.9 copy-done.16
  184.1 0.9 copy-done.18
  185.1 13.6 %grads.1 = (bf16[3,224,1024]{2,1,0:T(8,128)(2,1)}, bf16[3,224,1024]{2,1,0:T(8,128)(2,1)}) custom-call(bf16[1008,128]{1,0:T(8,128)(2,1)S(1)} %copy-done.6, bf16[1008,128]{1,0:T(8,128)(2,1)S(1)} %copy-done.16, bf16[1008,128]{1,0:T(8,128)(2,1)S(1)} %copy-done.18, bf16[1008,128]{1,0:T(8,128)(2,1)S(1)} %copy-done.14, ...), custom_call_target="tpu_custom_call" | custom-call | flops 2113929216 | bytes 10420224 | tf_op jit(solution)/shard_map/grads/pallas_call | solution.py:313
  198.7 1.2 shard_map.130
  (108 shorter events, 6.1 us)
Async XLA Ops:
  0.7 0.8 copy-start.20
  1.6 0.8 copy-start.21
  3.9 25.8 %copy-start.24 = (s32[224,192]{0,1:T(8,128)S(1)}, s32[224,192]{0,1:T(8,128)}, u32[]{:S(2)}) copy-start(s32[224,192]{0,1:T(8,128)} %param.15) | copy-start | bytes 516100
  4.6 11.4 %collective-permute-start.2 = (bf16[4,24,128]{2,1,0:T(8,128)(2,1)S(1)}, bf16[4,24,128]{2,1,0:T(8,128)(2,1)S(1)}, u32[]{:S(2)}, u32[]{:S(2)}) collective-permute-start(bf16[4,24,128]{2,1,0:T(8,128)(2,1)S(1)} %get-tuple-element.27), channel_id=1, source_target_pairs={{0,64},{64,128},{128,192},{192,0},{1,65},{65,129},{129,193},{193,1... | collective-permute-start | bytes 73736 | tf_op jit(solution)/shard_map/ppermute | solution.py:30
  7.9 8.1 %collective-permute-start = (bf16[4,24,128]{2,1,0:T(8,128)(2,1)S(1)}, bf16[4,24,128]{2,1,0:T(8,128)(2,1)S(1)}, u32[]{:S(2)}, u32[]{:S(2)}) collective-permute-start(bf16[4,24,128]{2,1,0:T(8,128)(2,1)S(1)} %get-tuple-element.29), channel_id=1, source_target_pairs={{0,192},{64,0},{128,64},{192,128},{1,193},{65,1},{129,65},{193,129... | collective-permute-start | bytes 73736 | tf_op jit(solution)/shard_map/ppermute | solution.py:30
  11.0 7.7 %collective-permute-start.1 = (bf16[4,24,128]{2,1,0:T(8,128)(2,1)S(1)}, bf16[4,24,128]{2,1,0:T(8,128)(2,1)S(1)}, u32[]{:S(2)}, u32[]{:S(2)}) collective-permute-start(bf16[4,24,128]{2,1,0:T(8,128)(2,1)S(1)} %get-tuple-element.28), channel_id=1, source_target_pairs={{0,128},{64,192},{128,0},{192,64},{1,129},{65,193},{129,1},{193,65... | collective-permute-start | bytes 73736 | tf_op jit(solution)/shard_map/ppermute | solution.py:30
  18.8 4.7 %collective-permute-start.3 = (bf16[4,4,24,128]{3,2,1,0:T(8,128)(2,1)S(1)}, bf16[4,4,24,128]{3,2,1,0:T(8,128)(2,1)S(1)}, u32[]{:S(2)}, u32[]{:S(2)}) collective-permute-start(bf16[4,4,24,128]{3,2,1,0:T(8,128)(2,1)S(1)} %get-tuple-element.24), channel_id=1, source_target_pairs={{0,32},{32,0},{1,33},{33,1},{2,34},{34,2},{3,35},{35,3},{4,36},{36... | collective-permute-start | bytes 294920 | tf_op jit(solution)/shard_map/ppermute | solution.py:352
  23.5 11.2 %collective-permute-start.14 = (bf16[2,2,4,24,128]{4,3,2,1,0:T(8,128)(2,1)S(1)}, bf16[2,2,4,24,128]{4,3,2,1,0:T(8,128)(2,1)S(1)}, u32[]{:S(2)}, u32[]{:S(2)}) collective-permute-start(bf16[2,2,4,24,128]{4,3,2,1,0:T(8,128)(2,1)S(1)} %get-tuple-element.22), channel_id=1, source_target_pairs={{0,24},{8,0},{16,8},{24,16},{1,25},{9,1},{17,9},{25,17},{2,26},{10... | collective-permute-start | bytes 294920 | tf_op jit(solution)/shard_map/ppermute | solution.py:30
  24.0 11.5 %collective-permute-start.15 = (bf16[2,2,4,24,128]{4,3,2,1,0:T(8,128)(2,1)S(1)}, bf16[2,2,4,24,128]{4,3,2,1,0:T(8,128)(2,1)S(1)}, u32[]{:S(2)}, u32[]{:S(2)}) collective-permute-start(bf16[2,2,4,24,128]{4,3,2,1,0:T(8,128)(2,1)S(1)} %get-tuple-element.22), channel_id=1, source_target_pairs={{0,16},{8,24},{16,0},{24,8},{1,17},{9,25},{17,1},{25,9},{2,18},{10... | collective-permute-start | bytes 294920 | tf_op jit(solution)/shard_map/ppermute | solution.py:30
  26.6 9.8 %collective-permute-start.16 = (bf16[2,2,4,24,128]{4,3,2,1,0:T(8,128)(2,1)S(1)}, bf16[2,2,4,24,128]{4,3,2,1,0:T(8,128)(2,1)S(1)}, u32[]{:S(2)}, u32[]{:S(2)}) collective-permute-start(bf16[2,2,4,24,128]{4,3,2,1,0:T(8,128)(2,1)S(1)} %get-tuple-element.22), channel_id=1, source_target_pairs={{0,8},{8,16},{16,24},{24,0},{1,9},{9,17},{17,25},{25,1},{2,10},{10... | collective-permute-start | bytes 294920 | tf_op jit(solution)/shard_map/ppermute | solution.py:30
  29.7 37.7 %copy-start.3 = (bf16[3,224,1024]{2,1,0:T(8,128)(2,1)S(1)}, bf16[3,224,1024]{2,1,0:T(8,128)(2,1)}, u32[]{:S(2)}) copy-start(bf16[3,224,1024]{2,1,0:T(8,128)(2,1)} %refs_10_.1) | copy-start | bytes 4128772
  29.9 37.5 %copy-start.19 = (bf16[3,224,1024]{2,1,0:T(8,128)(2,1)S(1)}, bf16[3,224,1024]{2,1,0:T(8,128)(2,1)}, u32[]{:S(2)}) copy-start(bf16[3,224,1024]{2,1,0:T(8,128)(2,1)} %s_ref.2) | copy-start | bytes 4128772
  30.5 12.8 %collective-permute-start.25 = (bf16[1008,128]{1,0:T(8,128)(2,1)S(1)}, bf16[1008,128]{1,0:T(8,128)(2,1)S(1)}, u32[]{:S(2)}, u32[]{:S(2)}) collective-permute-start(bf16[1008,128]{1,0:T(8,128)(2,1)S(1)} %shard_map.122.refs_5_.refs_4_), channel_id=1, source_target_pairs={{0,64},{64,128},{128,192},{192,0},{1,65},{65,129},{129,193},{193,1... | collective-permute-start | bytes 774152 | tf_op jit(solution)/shard_map/ppermute | solution.py:30
  32.0 6.4 %collective-permute-start.4 = (bf16[2,2,4,24,128]{4,3,2,1,0:T(8,128)(2,1)S(1)}, bf16[2,2,4,24,128]{4,3,2,1,0:T(8,128)(2,1)S(1)}, u32[]{:S(2)}, u32[]{:S(2)}) collective-permute-start(bf16[2,2,4,24,128]{4,3,2,1,0:T(8,128)(2,1)S(1)} %get-tuple-element.23), channel_id=1, source_target_pairs={{0,6},{2,0},{4,2},{6,4},{1,7},{3,1},{5,3},{7,5},{8,14},{10,8},{12,... | collective-permute-start | bytes 294920 | tf_op jit(solution)/shard_map/ppermute | solution.py:30
  34.7 7.2 %collective-permute-start.5 = (bf16[2,2,4,24,128]{4,3,2,1,0:T(8,128)(2,1)S(1)}, bf16[2,2,4,24,128]{4,3,2,1,0:T(8,128)(2,1)S(1)}, u32[]{:S(2)}, u32[]{:S(2)}) collective-permute-start(bf16[2,2,4,24,128]{4,3,2,1,0:T(8,128)(2,1)S(1)} %get-tuple-element.23), channel_id=1, source_target_pairs={{0,4},{2,6},{4,0},{6,2},{1,5},{3,7},{5,1},{7,3},{8,12},{10,14},{12... | collective-permute-start | bytes 294920 | tf_op jit(solution)/shard_map/ppermute | solution.py:30
  35.5 7.6 %collective-permute-start.6 = (bf16[2,2,4,24,128]{4,3,2,1,0:T(8,128)(2,1)S(1)}, bf16[2,2,4,24,128]{4,3,2,1,0:T(8,128)(2,1)S(1)}, u32[]{:S(2)}, u32[]{:S(2)}) collective-permute-start(bf16[2,2,4,24,128]{4,3,2,1,0:T(8,128)(2,1)S(1)} %get-tuple-element.23), channel_id=1, source_target_pairs={{0,2},{2,4},{4,6},{6,0},{1,3},{3,5},{5,7},{7,1},{8,10},{10,12},{12... | collective-permute-start | bytes 294920 | tf_op jit(solution)/shard_map/ppermute | solution.py:30
  36.5 10.8 %collective-permute-start.18 = (bf16[4,2,2,4,24,128]{5,4,3,2,1,0:T(8,128)(2,1)S(1)}, bf16[4,2,2,4,24,128]{5,4,3,2,1,0:T(8,128)(2,1)S(1)}, u32[]{:S(2)}, u32[]{:S(2)}) collective-permute-start(bf16[4,2,2,4,24,128]{5,4,3,2,1,0:T(8,128)(2,1)S(1)} %pad_maximum_fusion.2.refs_8_), channel_id=1, source_target_pairs={{0,2},{2,4},{4,6},{6,0},{1,3},{3,5},{5,7},{7,1},{8,10},{10,12},{12... | collective-permute-start | bytes 1179656 | tf_op jit(solution)/shard_map/ppermute | solution.py:30
  38.4 9.0 %collective-permute-start.17 = (bf16[4,2,2,4,24,128]{5,4,3,2,1,0:T(8,128)(2,1)S(1)}, bf16[4,2,2,4,24,128]{5,4,3,2,1,0:T(8,128)(2,1)S(1)}, u32[]{:S(2)}, u32[]{:S(2)}) collective-permute-start(bf16[4,2,2,4,24,128]{5,4,3,2,1,0:T(8,128)(2,1)S(1)} %pad_maximum_fusion.2.refs_8_), channel_id=1, source_target_pairs={{0,6},{2,0},{4,2},{6,4},{1,7},{3,1},{5,3},{7,5},{8,14},{10,8},{12,... | collective-permute-start | bytes 1179656 | tf_op jit(solution)/shard_map/ppermute | solution.py:30
  41.9 5.4 %collective-permute-start.20 = (bf16[4,2,2,4,24,128]{5,4,3,2,1,0:T(8,128)(2,1)S(1)}, bf16[4,2,2,4,24,128]{5,4,3,2,1,0:T(8,128)(2,1)S(1)}, u32[]{:S(2)}, u32[]{:S(2)}) collective-permute-start(bf16[4,2,2,4,24,128]{5,4,3,2,1,0:T(8,128)(2,1)S(1)} %pad_maximum_fusion.2.refs_8_), channel_id=1, source_target_pairs={{0,1},{1,0},{2,3},{3,2},{4,5},{5,4},{6,7},{7,6},{8,9},{9,8},{10,11... | collective-permute-start | bytes 1179656 | tf_op jit(solution)/shard_map/ppermute | solution.py:184
  43.2 10.4 %collective-permute-start.8 = (bf16[4,2,2,4,24,128]{5,4,3,2,1,0:T(8,128)(2,1)S(1)}, bf16[4,2,2,4,24,128]{5,4,3,2,1,0:T(8,128)(2,1)S(1)}, u32[]{:S(2)}, u32[]{:S(2)}) collective-permute-start(bf16[4,2,2,4,24,128]{5,4,3,2,1,0:T(8,128)(2,1)S(1)} %pad_maximum_fusion.1.refs_0_), channel_id=1, source_target_pairs={{0,8},{8,16},{16,24},{24,0},{1,9},{9,17},{17,25},{25,1},{2,10},{10... | collective-permute-start | bytes 1179656 | tf_op jit(solution)/shard_map/ppermute | solution.py:30
  43.3 84.8 %copy-start.7 = (bf16[1008,128]{1,0:T(8,128)(2,1)}, bf16[1008,128]{1,0:T(8,128)(2,1)S(1)}, u32[]{:S(2)}) copy-start(bf16[1008,128]{1,0:T(8,128)(2,1)S(1)} %collective-permute-done.25.refs_6_.refs_7_) | copy-start | bytes 774148
  43.3 10.5 %collective-permute-start.7 = (bf16[4,2,2,4,24,128]{5,4,3,2,1,0:T(8,128)(2,1)S(1)}, bf16[4,2,2,4,24,128]{5,4,3,2,1,0:T(8,128)(2,1)S(1)}, u32[]{:S(2)}, u32[]{:S(2)}) collective-permute-start(bf16[4,2,2,4,24,128]{5,4,3,2,1,0:T(8,128)(2,1)S(1)} %pad_maximum_fusion.1.refs_0_), channel_id=1, source_target_pairs={{0,24},{8,0},{16,8},{24,16},{1,25},{9,1},{17,9},{25,17},{2,26},{10... | collective-permute-start | bytes 1179656 | tf_op jit(solution)/shard_map/ppermute | solution.py:30
  47.3 6.5 %collective-permute-start.10 = (bf16[4,2,2,4,24,128]{5,4,3,2,1,0:T(8,128)(2,1)S(1)}, bf16[4,2,2,4,24,128]{5,4,3,2,1,0:T(8,128)(2,1)S(1)}, u32[]{:S(2)}, u32[]{:S(2)}) collective-permute-start(bf16[4,2,2,4,24,128]{5,4,3,2,1,0:T(8,128)(2,1)S(1)} %pad_maximum_fusion.1.refs_0_), channel_id=1, source_target_pairs={{0,1},{1,0},{2,3},{3,2},{4,5},{5,4},{6,7},{7,6},{8,9},{9,8},{10,11... | collective-permute-start | bytes 1179656 | tf_op jit(solution)/shard_map/ppermute | solution.py:184
  47.3 12.7 %collective-permute-start.19 = (bf16[4,2,2,4,24,128]{5,4,3,2,1,0:T(8,128)(2,1)S(1)}, bf16[4,2,2,4,24,128]{5,4,3,2,1,0:T(8,128)(2,1)S(1)}, u32[]{:S(2)}, u32[]{:S(2)}) collective-permute-start(bf16[4,2,2,4,24,128]{5,4,3,2,1,0:T(8,128)(2,1)S(1)} %collective-permute-done.18.refs_11_), channel_id=1, source_target_pairs={{0,2},{2,4},{4,6},{6,0},{1,3},{3,5},{5,7},{7,1},{8,10},{10,12},{12... | collective-permute-start | bytes 1179656 | tf_op jit(solution)/shard_map/ppermute | solution.py:30
  47.3 12.7 %collective-permute-start.21 = (bf16[4,2,2,4,24,128]{5,4,3,2,1,0:T(8,128)(2,1)S(1)}, bf16[4,2,2,4,24,128]{5,4,3,2,1,0:T(8,128)(2,1)S(1)}, u32[]{:S(2)}, u32[]{:S(2)}) collective-permute-start(bf16[4,2,2,4,24,128]{5,4,3,2,1,0:T(8,128)(2,1)S(1)} %collective-permute-done.17.refs_9_), channel_id=1, source_target_pairs={{0,1},{1,0},{2,3},{3,2},{4,5},{5,4},{6,7},{7,6},{8,9},{9,8},{10,11... | collective-permute-start | bytes 1179656 | tf_op jit(solution)/shard_map/ppermute | solution.py:184
  53.6 9.5 %collective-permute-start.9 = (bf16[4,2,2,4,24,128]{5,4,3,2,1,0:T(8,128)(2,1)S(1)}, bf16[4,2,2,4,24,128]{5,4,3,2,1,0:T(8,128)(2,1)S(1)}, u32[]{:S(2)}, u32[]{:S(2)}) collective-permute-start(bf16[4,2,2,4,24,128]{5,4,3,2,1,0:T(8,128)(2,1)S(1)} %collective-permute-done.8.refs_3_), channel_id=1, source_target_pairs={{0,8},{8,16},{16,24},{24,0},{1,9},{9,17},{17,25},{25,1},{2,10},{10... | collective-permute-start | bytes 1179656 | tf_op jit(solution)/shard_map/ppermute | solution.py:30
  53.9 9.2 %collective-permute-start.23 = (bf16[4,2,2,4,24,128]{5,4,3,2,1,0:T(8,128)(2,1)S(1)}, bf16[4,2,2,4,24,128]{5,4,3,2,1,0:T(8,128)(2,1)S(1)}, u32[]{:S(2)}, u32[]{:S(2)}) collective-permute-start(bf16[4,2,2,4,24,128]{5,4,3,2,1,0:T(8,128)(2,1)S(1)} %collective-permute-done.18.refs_11_), channel_id=1, source_target_pairs={{0,1},{1,0},{2,3},{3,2},{4,5},{5,4},{6,7},{7,6},{8,9},{9,8},{10,11... | collective-permute-start | bytes 1179656 | tf_op jit(solution)/shard_map/ppermute | solution.py:184
  53.9 14.0 %collective-permute-start.13 = (bf16[4,2,2,4,24,128]{5,4,3,2,1,0:T(8,128)(2,1)S(1)}, bf16[4,2,2,4,24,128]{5,4,3,2,1,0:T(8,128)(2,1)S(1)}, u32[]{:S(2)}, u32[]{:S(2)}) collective-permute-start(bf16[4,2,2,4,24,128]{5,4,3,2,1,0:T(8,128)(2,1)S(1)} %collective-permute-done.8.refs_3_), channel_id=1, source_target_pairs={{0,1},{1,0},{2,3},{3,2},{4,5},{5,4},{6,7},{7,6},{8,9},{9,8},{10,11... | collective-permute-start | bytes 1179656 | tf_op jit(solution)/shard_map/ppermute | solution.py:184
  60.1 7.7 %collective-permute-start.11 = (bf16[4,2,2,4,24,128]{5,4,3,2,1,0:T(8,128)(2,1)S(1)}, bf16[4,2,2,4,24,128]{5,4,3,2,1,0:T(8,128)(2,1)S(1)}, u32[]{:S(2)}, u32[]{:S(2)}) collective-permute-start(bf16[4,2,2,4,24,128]{5,4,3,2,1,0:T(8,128)(2,1)S(1)} %collective-permute-done.7.refs_1_), channel_id=1, source_target_pairs={{0,1},{1,0},{2,3},{3,2},{4,5},{5,4},{6,7},{7,6},{8,9},{9,8},{10,11... | collective-permute-start | bytes 1179656 | tf_op jit(solution)/shard_map/ppermute | solution.py:184
  60.1 7.8 %collective-permute-start.22 = (bf16[4,2,2,4,24,128]{5,4,3,2,1,0:T(8,128)(2,1)S(1)}, bf16[4,2,2,4,24,128]{5,4,3,2,1,0:T(8,128)(2,1)S(1)}, u32[]{:S(2)}, u32[]{:S(2)}) collective-permute-start(bf16[4,2,2,4,24,128]{5,4,3,2,1,0:T(8,128)(2,1)S(1)} %collective-permute-done.19.refs_10_), channel_id=1, source_target_pairs={{0,1},{1,0},{2,3},{3,2},{4,5},{5,4},{6,7},{7,6},{8,9},{9,8},{10,11... | collective-permute-start | bytes 1179656 | tf_op jit(solution)/shard_map/ppermute | solution.py:184
  63.0 4.9 %collective-permute-start.12 = (bf16[4,2,2,4,24,128]{5,4,3,2,1,0:T(8,128)(2,1)S(1)}, bf16[4,2,2,4,24,128]{5,4,3,2,1,0:T(8,128)(2,1)S(1)}, u32[]{:S(2)}, u32[]{:S(2)}) collective-permute-start(bf16[4,2,2,4,24,128]{5,4,3,2,1,0:T(8,128)(2,1)S(1)} %collective-permute-done.9.refs_2_), channel_id=1, source_target_pairs={{0,1},{1,0},{2,3},{3,2},{4,5},{5,4},{6,7},{7,6},{8,9},{9,8},{10,11... | collective-permute-start | bytes 1179656 | tf_op jit(solution)/shard_map/ppermute | solution.py:184
  63.0 15.5 %collective-permute-start.26 = (bf16[1008,128]{1,0:T(8,128)(2,1)S(1)}, bf16[1008,128]{1,0:T(8,128)(2,1)S(1)}, u32[]{:S(2)}, u32[]{:S(2)}) collective-permute-start(bf16[1008,128]{1,0:T(8,128)(2,1)S(1)} %collective-permute-done.25.refs_6_.refs_7_), channel_id=1, source_target_pairs={{0,64},{64,128},{128,192},{192,0},{1,65},{65,129},{129,193},{193,1... | collective-permute-start | bytes 774152 | tf_op jit(solution)/shard_map/ppermute | solution.py:30
  67.8 10.8 %copy-start.2 = (bf16[3,224,1024]{2,1,0:T(8,128)(2,1)S(1)}, bf16[3,224,1024]{2,1,0:T(8,128)(2,1)}, u32[]{:S(2)}) copy-start(bf16[3,224,1024]{2,1,0:T(8,128)(2,1)} %refs_2_.5) | copy-start | bytes 4128772
  67.8 17.1 %collective-permute-start.24 = (bf16[1008,128]{1,0:T(8,128)(2,1)S(1)}, bf16[1008,128]{1,0:T(8,128)(2,1)S(1)}, u32[]{:S(2)}, u32[]{:S(2)}) collective-permute-start(bf16[1008,128]{1,0:T(8,128)(2,1)S(1)} %shard_map.122.refs_5_.refs_4_), channel_id=1, source_target_pairs={{0,192},{64,0},{128,64},{192,128},{1,193},{65,1},{129,65},{193,129... | collective-permute-start | bytes 774152 | tf_op jit(solution)/shard_map/ppermute | solution.py:30
  73.8 21.3 %copy-start = (bf16[2,4,192,1024]{3,2,1,0:T(8,128)(2,1)}, bf16[2,4,192,1024]{3,2,1,0:T(8,128)(2,1)S(1)}, u32[]{:S(2)}) copy-start(bf16[2,4,192,1024]{3,2,1,0:T(8,128)(2,1)S(1)} %get-tuple-element.11.refs_1_.refs_8_) | copy-start | bytes 9437188
  78.6 54.6 %copy-start.11 = (bf16[1008,128]{1,0:T(8,128)(2,1)}, bf16[1008,128]{1,0:T(8,128)(2,1)S(1)}, u32[]{:S(2)}) copy-start(bf16[1008,128]{1,0:T(8,128)(2,1)S(1)} %collective-permute-done.26.refs_5_.refs_6_) | copy-start | bytes 774148
  80.7 10.3 %collective-permute-start.27 = (bf16[504,128]{1,0:T(8,128)(2,1)S(1)}, bf16[504,128]{1,0:T(8,128)(2,1)S(1)}, u32[]{:S(2)}, u32[]{:S(2)}) collective-permute-start(bf16[504,128]{1,0:T(8,128)(2,1)S(1)} %get-tuple-element.21), channel_id=1, source_target_pairs={{0,64},{64,128},{128,192},{192,0},{1,65},{65,129},{129,193},{193,1... | collective-permute-start | bytes 387080 | tf_op jit(solution)/shard_map/ppermute | solution.py:30
  84.2 7.5 %collective-permute-start.29 = (bf16[504,128]{1,0:T(8,128)(2,1)S(1)}, bf16[504,128]{1,0:T(8,128)(2,1)S(1)}, u32[]{:S(2)}, u32[]{:S(2)}) collective-permute-start(bf16[504,128]{1,0:T(8,128)(2,1)S(1)} %get-tuple-element.20), channel_id=1, source_target_pairs={{0,192},{64,0},{128,64},{192,128},{1,193},{65,1},{129,65},{193,129... | collective-permute-start | bytes 387080 | tf_op jit(solution)/shard_map/ppermute | solution.py:30
  84.9 43.3 %copy-start.9 = (bf16[1008,128]{1,0:T(8,128)(2,1)}, bf16[1008,128]{1,0:T(8,128)(2,1)S(1)}, u32[]{:S(2)}) copy-start(bf16[1008,128]{1,0:T(8,128)(2,1)S(1)} %collective-permute-done.24.refs_5_.refs_6_) | copy-start | bytes 774148
  91.8 14.2 %collective-permute-start.30 = (bf16[1008,128]{1,0:T(8,128)(2,1)S(1)}, bf16[1008,128]{1,0:T(8,128)(2,1)S(1)}, u32[]{:S(2)}, u32[]{:S(2)}) collective-permute-start(bf16[1008,128]{1,0:T(8,128)(2,1)S(1)} %pad_maximum_fusion.4), channel_id=1, source_target_pairs={{0,192},{64,0},{128,64},{192,128},{1,193},{65,1},{129,65},{193,129... | collective-permute-start | bytes 774152 | tf_op jit(solution)/shard_map/ppermute | solution.py:30
  93.9 14.8 %collective-permute-start.28 = (bf16[1008,128]{1,0:T(8,128)(2,1)S(1)}, bf16[1008,128]{1,0:T(8,128)(2,1)S(1)}, u32[]{:S(2)}, u32[]{:S(2)}) collective-permute-start(bf16[1008,128]{1,0:T(8,128)(2,1)S(1)} %pad_maximum_fusion.3), channel_id=1, source_target_pairs={{0,64},{64,128},{128,192},{192,0},{1,65},{65,129},{129,193},{193,1... | collective-permute-start | bytes 774152 | tf_op jit(solution)/shard_map/ppermute | solution.py:30
  109.4 6.9 %copy-start.5 = (bf16[1008,128]{1,0:T(8,128)(2,1)}, bf16[1008,128]{1,0:T(8,128)(2,1)S(1)}, u32[]{:S(2)}) copy-start(bf16[1008,128]{1,0:T(8,128)(2,1)S(1)} %shard_map.126.refs_4_.refs_0_) | copy-start | bytes 774148
  109.5 14.4 %collective-permute-start.33 = (bf16[1008,128]{1,0:T(8,128)(2,1)S(1)}, bf16[1008,128]{1,0:T(8,128)(2,1)S(1)}, u32[]{:S(2)}, u32[]{:S(2)}) collective-permute-start(bf16[1008,128]{1,0:T(8,128)(2,1)S(1)} %shard_map.126.refs_4_.refs_0_), channel_id=1, source_target_pairs={{0,64},{64,128},{128,192},{192,0},{1,65},{65,129},{129,193},{193,1... | collective-permute-start | bytes 774152 | tf_op jit(solution)/shard_map/ppermute | solution.py:30
  109.5 14.4 %collective-permute-start.32 = (bf16[1008,128]{1,0:T(8,128)(2,1)S(1)}, bf16[1008,128]{1,0:T(8,128)(2,1)S(1)}, u32[]{:S(2)}, u32[]{:S(2)}) collective-permute-start(bf16[1008,128]{1,0:T(8,128)(2,1)S(1)} %shard_map.126.refs_4_.refs_0_), channel_id=1, source_target_pairs={{0,192},{64,0},{128,64},{192,128},{1,193},{65,1},{129,65},{193,129... | collective-permute-start | bytes 774152 | tf_op jit(solution)/shard_map/ppermute | solution.py:30
  116.4 20.1 %collective-permute-start.31 = (bf16[32,1,2,24,128]{4,3,2,1,0:T(8,128)(2,1)S(1)}, bf16[32,1,2,24,128]{4,3,2,1,0:T(8,128)(2,1)S(1)}, u32[]{:S(2)}, u32[]{:S(2)}) collective-permute-start(bf16[32,1,2,24,128]{4,3,2,1,0:T(8,128)(2,1)S(1)} %slice_bitcast_fusion.4), channel_id=1, source_target_pairs={{0,1},{1,0},{2,3},{3,2},{4,5},{5,4},{6,7},{7,6},{8,9},{9,8},{10,11... | collective-permute-start | bytes 1179656 | tf_op jit(solution)/shard_map/ppermute | solution.py:329
  123.9 9.0 %copy-start.13 = (bf16[1008,128]{1,0:T(8,128)(2,1)}, bf16[1008,128]{1,0:T(8,128)(2,1)S(1)}, u32[]{:S(2)}) copy-start(bf16[1008,128]{1,0:T(8,128)(2,1)S(1)} %collective-permute-done.33.refs_5_.refs_3_) | copy-start | bytes 774148
  123.9 9.2 %collective-permute-start.35 = (bf16[504,128]{1,0:T(8,128)(2,1)S(1)}, bf16[504,128]{1,0:T(8,128)(2,1)S(1)}, u32[]{:S(2)}, u32[]{:S(2)}) collective-permute-start(bf16[504,128]{1,0:T(8,128)(2,1)S(1)} %slice.120), channel_id=1, source_target_pairs={{0,64},{64,128},{128,192},{192,0},{1,65},{65,129},{129,193},{193,1... | collective-permute-start | bytes 387080 | tf_op jit(solution)/shard_map/ppermute | solution.py:30
  124.0 8.9 %copy-start.15 = (bf16[1008,128]{1,0:T(8,128)(2,1)}, bf16[1008,128]{1,0:T(8,128)(2,1)S(1)}, u32[]{:S(2)}) copy-start(bf16[1008,128]{1,0:T(8,128)(2,1)S(1)} %collective-permute-done.32.refs_4_.refs_1_) | copy-start | bytes 774148
  124.0 9.1 %collective-permute-start.36 = (bf16[504,128]{1,0:T(8,128)(2,1)S(1)}, bf16[504,128]{1,0:T(8,128)(2,1)S(1)}, u32[]{:S(2)}, u32[]{:S(2)}) collective-permute-start(bf16[504,128]{1,0:T(8,128)(2,1)S(1)} %slice.121), channel_id=1, source_target_pairs={{0,192},{64,0},{128,64},{192,128},{1,193},{65,1},{129,65},{193,129... | collective-permute-start | bytes 387080 | tf_op jit(solution)/shard_map/ppermute | solution.py:30
  133.0 4.9 %collective-permute-start.34 = (bf16[32,2,2,24,128]{4,3,2,1,0:T(8,128)(2,1)S(1)}, bf16[32,2,2,24,128]{4,3,2,1,0:T(8,128)(2,1)S(1)}, u32[]{:S(2)}, u32[]{:S(2)}) collective-permute-start(bf16[32,2,2,24,128]{4,3,2,1,0:T(8,128)(2,1)S(1)} %slice_bitcast_fusion), channel_id=1, source_target_pairs={{0,1},{1,0},{2,3},{3,2},{4,5},{5,4},{6,7},{7,6},{8,9},{9,8},{10,11... | collective-permute-start | bytes 2359304 | tf_op jit(solution)/shard_map/ppermute | solution.py:329
  133.2 2.6 %copy-start.17 = (bf16[1008,128]{1,0:T(8,128)(2,1)}, bf16[1008,128]{1,0:T(8,128)(2,1)S(1)}, u32[]{:S(2)}) copy-start(bf16[1008,128]{1,0:T(8,128)(2,1)S(1)} %constant_dynamic-update-slice_fusion.refs_4_.refs_2_) | copy-start | bytes 774148
  135.8 1.9 collective-permute-start.37
  168.2 30.5 %collective-permute-start.38 = (bf16[48,128]{1,0:T(8,128)(2,1)S(1)}, bf16[48,128]{1,0:T(8,128)(2,1)S(1)}, u32[]{:S(2)}, u32[]{:S(2)}) collective-permute-start(bf16[48,128]{1,0:T(8,128)(2,1)S(1)} %get-tuple-element.32), channel_id=1, source_target_pairs={{0,192},{64,0},{128,64},{192,128},{1,193},{65,1},{129,65},{193,129... | collective-permute-start | bytes 36872 | tf_op jit(solution)/shard_map/ppermute | solution.py:30
  171.3 27.4 %collective-permute-start.39 = (bf16[48,128]{1,0:T(8,128)(2,1)S(1)}, bf16[48,128]{1,0:T(8,128)(2,1)S(1)}, u32[]{:S(2)}, u32[]{:S(2)}) collective-permute-start(bf16[48,128]{1,0:T(8,128)(2,1)S(1)} %get-tuple-element.31), channel_id=1, source_target_pairs={{0,128},{64,192},{128,0},{192,64},{1,129},{65,193},{129,1},{193,65... | collective-permute-start | bytes 36872 | tf_op jit(solution)/shard_map/ppermute | solution.py:30
  175.2 23.5 %collective-permute-start.40 = (bf16[48,128]{1,0:T(8,128)(2,1)S(1)}, bf16[48,128]{1,0:T(8,128)(2,1)S(1)}, u32[]{:S(2)}, u32[]{:S(2)}) collective-permute-start(bf16[48,128]{1,0:T(8,128)(2,1)S(1)} %get-tuple-element.30), channel_id=1, source_target_pairs={{0,64},{64,128},{128,192},{192,0},{1,65},{65,129},{129,193},{193,1... | collective-permute-start | bytes 36872 | tf_op jit(solution)/shard_map/ppermute | solution.py:30
  175.2 1.9 copy-start.1
  177.1 1.3 copy-start.4
  178.4 0.9 copy-start.6
  179.4 0.9 copy-start.8
  180.3 0.9 copy-start.10
  181.3 0.9 copy-start.12
  182.2 0.9 copy-start.14
  183.2 0.9 copy-start.16
  184.1 0.9 copy-start.18
  (2 other events, 1.5 us)
where the time goes:
time: 201 us; the launch traced here: 200 us
  starting transfers between devices  59.9 us (30%)
  waiting for transfers between devices  52.6 us (26%)
  Pallas kernels  40.8 us (20%)
  blocking collectives  28.3 us (14%)
  local copies, waits for them, and re-layouts  14.8 us (7%)
  other arithmetic  2.49 us (1%)
    ppermute x29, starting transfers between devices, shift(): return lax.ppermute(x, axis, [(i, (i + by) % 4) for i in range(4)])  56.4 us
    ppermute x29, waiting for transfers between devices, shift(): return lax.ppermute(x, axis, [(i, (i + by) % 4) for i in range(4)])  47.7 us
    all_to_all x1, blocking collectives, a2a(): return lax.all_to_all(x, axes, split_axis=0, concat_axis=0, tiled=True)  28.3 us
    pallas_call x11, Pallas kernels, on_chip_call(): pl.pallas_call(body, in_specs=[SCALARS] + [ON_CHIP] * (len(args) - 1), ou...  26.8 us
    unnamed x53, local copies, waits for them, and re-layouts  14.4 us
    pallas_call x1, Pallas kernels, grads(): pl.pallas_call(grads_body, grid=(4,), in_specs=[ON_CHIP] * 8 + [group] *...  13.6 us
  transfers between devices with their start and end apart: 41, of which 15 were waited for; matrix products, arithmetic and copies ran while one was open for 1% of the time, Pallas kernels for 19%

commit v1 on v0

--- a/solution.py
+++ b/solution.py
@@ -161,7 +161,7 @@
                                 both[a, at] = ref[i, z, a, g].astype(F32)
                         return carry
 
-                    lax.fori_loop(0, 4, place, 0)
+                    lax.fori_loop(0, 4, place, 0, unroll=True)
             for a, o_ref in ((0, plain_ref), (1, sign_ref)):
                 for j in range(8):
                     o_ref[src, g, :, j * 128 : (j + 1) * 128] = both[a, pl.ds(j, T, stride=8)].astype(BF)
@@ -192,21 +192,29 @@
     return pl.ds(pl.multiple_of(k * PK, 16), PK)
 
 
+def split_step(step, rels):
+    i = jnp.where(step >= 3, 1, 0)
+    return i, rels[0] + i * (rels[-1] - rels[0]), step - 3 * i
+
+
 def project_body(rels, pos, x_ref, a_ref, m_ref, p_ref, *refs):
-    s_refs, o_ref = refs[:-1], refs[-1]
-    for i, rel in enumerate(rels):
-
-        def one(k, carry):
-            plain = x_ref[k >> 1, rel]
-            flip = plain * a_ref[k >> 1, rel]
-            mean = pack(nt(m_ref[k], plain))
-            pert = pack(nt(p_ref[k], flip))
-            sign = s_refs[i][packed_rows(k)].astype(F32)
-            scale = scale_of(k)
-            o_ref[i, packed_rows(k)] = (scale * mean + scale * pert * sign).astype(BF)
-            return carry
-
-        lax.fori_loop(0, 3, one, 0)
+    n = len(rels)
+    s_refs, o_ref, signs = refs[:n], refs[n], refs[n + 1]
+    for i in range(n):
+        signs[i] = s_refs[i][...]
+
+    def one(step, carry):
+        i, rel, k = split_step(step, rels)
+        plain = x_ref[k >> 1, rel]
+        flip = plain * a_ref[k >> 1, rel]
+        mean = pack(nt(m_ref[k], plain))
+        pert = pack(nt(p_ref[k], flip))
+        sign = signs[i, packed_rows(k)].astype(F32)
+        scale = scale_of(k)
+        o_ref[i, packed_rows(k)] = (scale * mean + scale * pert * sign).astype(BF)
+        return carry
+
+    lax.fori_loop(0, 3 * n, one, 0)
 
 
 def project(pos, acts, means, perturb, signs, rels):
@@ -214,6 +222,7 @@
         lambda *refs: project_body(rels, *refs),
         [pos, *acts, means, perturb, *(signs[rel] for rel in rels)],
         [(len(rels), 3 * PK, 128)],
+        scratch=[pltpu.VMEM((len(rels), 3 * PK, 128), BF)],
         flops=len(rels) * 12 * F * W * T,
     )[0]
 
@@ -236,33 +245,36 @@
 
 def back_body(rels, pos, a_ref, m_ref, p_ref, *refs):
     n = len(rels)
-    h_refs, s_refs, o_ref, rows = refs[:n], refs[n : 2 * n], refs[2 * n], refs[2 * n + 1]
+    o_ref, rows, acts, signs = refs[2 * n :]
     c = pos[4]
-    for i, rel in enumerate(rels):
-
-        def one(k, carry):
-            h = h_refs[i][packed_rows(k)]
-            mean = tn(unpack(h), m_ref[k])
-            pert = tn(unpack(h * s_refs[i][packed_rows(k)]), p_ref[k])
-            scale = scale_of(k)
-            v = scale * mean + scale * pert * a_ref[k >> 1, rel].astype(F32)
-            for q in range(8):
-                at = pl.ds(q, T, stride=8)
-                before = jnp.where(k == 1, rows[k >> 1, at], 0.0)
-                rows[k >> 1, at] = before + v[:, q * 128 : (q + 1) * 128]
-            return carry
-
-        lax.fori_loop(0, 3, one, 0)
-
-        def place(q, carry):
+    for i in range(n):
+        acts[i], signs[i] = refs[i][...], refs[n + i][...]
+
+    def one(step, carry):
+        i, rel, k = split_step(step, rels)
+        h = acts[i, packed_rows(k)]
+        mean = tn(unpack(h), m_ref[k])
+        pert = tn(unpack(h * signs[i, packed_rows(k)]), p_ref[k])
+        scale = scale_of(k)
+        v = scale * mean + scale * pert * a_ref[k >> 1, rel].astype(F32)
+        for q in range(8):
+            at = pl.ds(q, T, stride=8)
+            before = jnp.where(k == 1, rows[i, k >> 1, at], 0.0)
+            rows[i, k >> 1, at] = before + v[:, q * 128 : (q + 1) * 128]
+        return carry
+
+    lax.fori_loop(0, 3 * n, one, 0)
+
+    def place(q, carry):
+        for i in range(n):
             for j in range(2):
                 for col in range(2):
                     at = pl.multiple_of(q * 48 + col * 24, 8)
                     half = c if col == 0 else 1 - c
-                    o_ref[half, q, i, j] = rows[1 - j, pl.ds(at, 24)].astype(BF)
-            return carry
-
-        lax.fori_loop(0, 32, place, 0)
+                    o_ref[half, q, i, j] = rows[i, 1 - j, pl.ds(at, 24)].astype(BF)
+        return carry
+
+    lax.fori_loop(0, 32, place, 0, unroll=2)
 
 
 def back(pos, h, signs, a, means, perturb, rels):
@@ -270,7 +282,8 @@
         lambda *refs: back_body(rels, *refs),
         [pos, a, means, perturb, *h, *(signs[rel] for rel in rels)],
         [(2, 32, len(rels), 2, 24, 128)],
-        scratch=[pltpu.VMEM((2, ROWS, 128), F32)],
+        scratch=[pltpu.VMEM((len(rels), 2, ROWS, 128), F32)]
+        + [pltpu.VMEM((len(rels), 3 * PK, 128), BF)] * 2,
         flops=len(rels) * 12 * F * W * T,
     )[0]
 
@@ -307,15 +320,16 @@
 
 
 def grads(h, signs, acts, noise):
-    w = pl.BlockSpec((3, F, 256), lambda i: (0, 0, i))
-    group = pl.BlockSpec((2, G, T, 256), lambda i: (0, 0, 0, i))
+    w = pl.BlockSpec((3, F, 512), lambda i: (0, 0, i))
+    group = pl.BlockSpec((2, G, T, 512), lambda i: (0, 0, 0, i))
+    packed = pl.BlockSpec((3 * PK, 128), lambda i: (0, 0))
     out = jax.ShapeDtypeStruct((3, F, W), BF)
     return pl.pallas_call(
         grads_body,
-        grid=(4,),
-        in_specs=[ON_CHIP] * 8 + [group] * 2 + [w],
+        grid=(2,),
+        in_specs=[packed] * 8 + [group] * 2 + [w],
         out_specs=[w, w],
-        scratch_shapes=[pltpu.VMEM((G, 6, F, T), BF), pltpu.VMEM((6, F, 256), F32)],
+        scratch_shapes=[pltpu.VMEM((G, 6, F, T), BF), pltpu.VMEM((6, F, 512), F32)],
         out_shape=[out, out],
         compiler_params=pltpu.CompilerParams(vmem_limit_bytes=28 * 1024 * 1024),
         cost_estimate=pl.CostEstimate(

time: 201 us -> 197 us (0.980)
  Pallas kernels: 40.8 us -> 34.6 us
    pallas_call x1, Pallas kernels: 13.6 us -> 9.54 us  [grads(): pl.pallas_call(grads_body, grid=(2,), in_specs=[packed] * 8 + [group] * 2...]
    pallas_call x11, Pallas kernels: 26.8 us -> 24.7 us  [on_chip_call(): pl.pallas_call(body, in_specs=[SCALARS] + [ON_CHIP] * (len(args) - 1), ou...]
  transfers between devices with their start and end apart: 41 -> 41, of which waited for: 15 -> 15; matrix products, arithmetic and copies ran while one was open for 1% -> 1% of each run, Pallas kernels for 19% -> 16%
where the time goes in v1:
time: 197 us; the launch traced here: 196 us
  starting transfers between devices  60.1 us (31%)
  waiting for transfers between devices  54.4 us (28%)
  Pallas kernels  34.6 us (18%)
  blocking collectives  28.3 us (14%)
  local copies, waits for them, and re-layouts  14.8 us (8%)
  other arithmetic  2.49 us (1%)
    ppermute x29, starting transfers between devices, shift(): return lax.ppermute(x, axis, [(i, (i + by) % 4) for i in range(4)])  56.6 us
    ppermute x29, waiting for transfers between devices, shift(): return lax.ppermute(x, axis, [(i, (i + by) % 4) for i in range(4)])  49.6 us
    all_to_all x1, blocking collectives, a2a(): return lax.all_to_all(x, axes, split_axis=0, concat_axis=0, tiled=True)  28.3 us
    pallas_call x11, Pallas kernels, on_chip_call(): pl.pallas_call(body, in_specs=[SCALARS] + [ON_CHIP] * (len(args) - 1), ou...  24.7 us
    unnamed x53, local copies, waits for them, and re-layouts  14.4 us
    pallas_call x1, Pallas kernels, grads(): pl.pallas_call(grads_body, grid=(2,), in_specs=[packed] * 8 + [group] * 2...  9.54 us
  transfers between devices with their start and end apart: 41, of which 15 were waited for; matrix products, arithmetic and copies ran while one was open for 1% of the time, Pallas kernels for 16%

profile of v1, /device:TPU:8, one launch (start us, length us, event | category | flops | bytes accessed | tf_op | source)
XLA Modules:
  0.0 195.8 jit_solution(5376221084623454662)
XLA Ops:
  0.7 0.8 copy-done.20
  1.6 0.8 copy-done.21
  2.4 0.8 copy-done.22
  3.2 0.8 copy-done.23
  4.6 3.3 %collective-permute-start.2 = (bf16[4,24,128]{2,1,0:T(8,128)(2,1)S(1)}, bf16[4,24,128]{2,1,0:T(8,128)(2,1)S(1)}, u32[]{:S(2)}, u32[]{:S(2)}) collective-permute-start(bf16[4,24,128]{2,1,0:T(8,128)(2,1)S(1)} %get-tuple-element.27), channel_id=1, source_target_pairs={{0,64},{64,128},{128,192},{192,0},{1,65},{65,129},{129,193},{193,1... | collective-permute-start | bytes 73736 | tf_op jit(solution)/shard_map/ppermute | solution.py:30
  7.9 3.1 %collective-permute-start = (bf16[4,24,128]{2,1,0:T(8,128)(2,1)S(1)}, bf16[4,24,128]{2,1,0:T(8,128)(2,1)S(1)}, u32[]{:S(2)}, u32[]{:S(2)}) collective-permute-start(bf16[4,24,128]{2,1,0:T(8,128)(2,1)S(1)} %get-tuple-element.29), channel_id=1, source_target_pairs={{0,192},{64,0},{128,64},{192,128},{1,193},{65,1},{129,65},{193,129... | collective-permute-start | bytes 73736 | tf_op jit(solution)/shard_map/ppermute | solution.py:30
  11.0 4.9 %collective-permute-start.1 = (bf16[4,24,128]{2,1,0:T(8,128)(2,1)S(1)}, bf16[4,24,128]{2,1,0:T(8,128)(2,1)S(1)}, u32[]{:S(2)}, u32[]{:S(2)}) collective-permute-start(bf16[4,24,128]{2,1,0:T(8,128)(2,1)S(1)} %get-tuple-element.28), channel_id=1, source_target_pairs={{0,128},{64,192},{128,0},{192,64},{1,129},{65,193},{129,1},{193,65... | collective-permute-start | bytes 73736 | tf_op jit(solution)/shard_map/ppermute | solution.py:30
  16.0 2.8 %collective-permute-done.1 = bf16[4,24,128]{2,1,0:T(8,128)(2,1)S(1)} collective-permute-done((bf16[4,24,128]{2,1,0:T(8,128)(2,1)S(1)}, bf16[4,24,128]{2,1,0:T(8,128)(2,1)S(1)}, u32[]{:S(2)}, u32[]{:S(2)}) %collective-permute-start.1) | collective-permute-done | bytes 24608 | tf_op jit(solution)/shard_map/ppermute | solution.py:30
  18.8 1.1 collective-permute-start.3
  19.9 3.6 %collective-permute-done.3 = bf16[4,4,24,128]{3,2,1,0:T(8,128)(2,1)S(1)} collective-permute-done((bf16[4,4,24,128]{3,2,1,0:T(8,128)(2,1)S(1)}, bf16[4,4,24,128]{3,2,1,0:T(8,128)(2,1)S(1)}, u32[]{:S(2)}, u32[]{:S(2)}) %collective-permute-start.3) | collective-permute-done | bytes 98336 | tf_op jit(solution)/shard_map/ppermute | solution.py:366
  24.0 2.6 %collective-permute-start.15 = (bf16[2,2,4,24,128]{4,3,2,1,0:T(8,128)(2,1)S(1)}, bf16[2,2,4,24,128]{4,3,2,1,0:T(8,128)(2,1)S(1)}, u32[]{:S(2)}, u32[]{:S(2)}) collective-permute-start(bf16[2,2,4,24,128]{4,3,2,1,0:T(8,128)(2,1)S(1)} %get-tuple-element.22), channel_id=1, source_target_pairs={{0,16},{8,24},{16,0},{24,8},{1,17},{9,25},{17,1},{25,9},{2,18},{10... | collective-permute-start | bytes 294920 | tf_op jit(solution)/shard_map/ppermute | solution.py:30
  26.6 1.9 collective-permute-start.16
  28.5 1.2 copy.13.s_ref
  29.9 0.6 shard_map.122.refs_5_.refs_4_
  30.5 1.4 collective-permute-start.25
  32.0 2.8 %collective-permute-start.4 = (bf16[2,2,4,24,128]{4,3,2,1,0:T(8,128)(2,1)S(1)}, bf16[2,2,4,24,128]{4,3,2,1,0:T(8,128)(2,1)S(1)}, u32[]{:S(2)}, u32[]{:S(2)}) collective-permute-start(bf16[2,2,4,24,128]{4,3,2,1,0:T(8,128)(2,1)S(1)} %get-tuple-element.23), channel_id=1, source_target_pairs={{0,6},{2,0},{4,2},{6,4},{1,7},{3,1},{5,3},{7,5},{8,14},{10,8},{12,... | collective-permute-start | bytes 294920 | tf_op jit(solution)/shard_map/ppermute | solution.py:30
  34.7 0.8 collective-permute-start.5
  35.5 0.9 collective-permute-start.6
  36.5 1.9 collective-permute-start.18
  38.4 2.4 %collective-permute-start.17 = (bf16[4,2,2,4,24,128]{5,4,3,2,1,0:T(8,128)(2,1)S(1)}, bf16[4,2,2,4,24,128]{5,4,3,2,1,0:T(8,128)(2,1)S(1)}, u32[]{:S(2)}, u32[]{:S(2)}) collective-permute-start(bf16[4,2,2,4,24,128]{5,4,3,2,1,0:T(8,128)(2,1)S(1)} %pad_maximum_fusion.2.refs_8_), channel_id=1, source_target_pairs={{0,6},{2,0},{4,2},{6,4},{1,7},{3,1},{5,3},{7,5},{8,14},{10,8},{12,... | collective-permute-start | bytes 1179656 | tf_op jit(solution)/shard_map/ppermute | solution.py:30
  40.8 1.1 collective-permute-done.5
  41.9 1.2 collective-permute-done.6
  43.3 1.9 collective-permute-start.7
  45.3 2.0 %collective-permute-done.18.refs_11_ = bf16[4,2,2,4,24,128]{5,4,3,2,1,0:T(8,128)(2,1)S(1)} collective-permute-done((bf16[4,2,2,4,24,128]{5,4,3,2,1,0:T(8,128)(2,1)S(1)}, bf16[4,2,2,4,24,128]{5,4,3,2,1,0:T(8,128)(2,1)S(1)}, u32[]{:S(2)}, u32[]{:S(2)}) %collective-permute-start.18) | collective-permute-done | bytes 393248 | tf_op jit(solution)/shard_map/ppermute | solution.py:30
  47.9 5.6 %collective-permute-done.8.refs_3_ = bf16[4,2,2,4,24,128]{5,4,3,2,1,0:T(8,128)(2,1)S(1)} collective-permute-done((bf16[4,2,2,4,24,128]{5,4,3,2,1,0:T(8,128)(2,1)S(1)}, bf16[4,2,2,4,24,128]{5,4,3,2,1,0:T(8,128)(2,1)S(1)}, u32[]{:S(2)}, u32[]{:S(2)}) %collective-permute-start.8) | collective-permute-done | bytes 393248 | tf_op jit(solution)/shard_map/ppermute | solution.py:30
  54.4 5.7 %collective-permute-done.19.refs_10_ = bf16[4,2,2,4,24,128]{5,4,3,2,1,0:T(8,128)(2,1)S(1)} collective-permute-done((bf16[4,2,2,4,24,128]{5,4,3,2,1,0:T(8,128)(2,1)S(1)}, bf16[4,2,2,4,24,128]{5,4,3,2,1,0:T(8,128)(2,1)S(1)}, u32[]{:S(2)}, u32[]{:S(2)}) %collective-permute-start.19) | collective-permute-done | bytes 393248 | tf_op jit(solution)/shard_map/ppermute | solution.py:30
  60.6 2.5 %collective-permute-done.9.refs_2_ = bf16[4,2,2,4,24,128]{5,4,3,2,1,0:T(8,128)(2,1)S(1)} collective-permute-done((bf16[4,2,2,4,24,128]{5,4,3,2,1,0:T(8,128)(2,1)S(1)}, bf16[4,2,2,4,24,128]{5,4,3,2,1,0:T(8,128)(2,1)S(1)}, u32[]{:S(2)}, u32[]{:S(2)}) %collective-permute-start.9) | collective-permute-done | bytes 393248 | tf_op jit(solution)/shard_map/ppermute | solution.py:30
  63.0 4.4 %collective-permute-start.26 = (bf16[1008,128]{1,0:T(8,128)(2,1)S(1)}, bf16[1008,128]{1,0:T(8,128)(2,1)S(1)}, u32[]{:S(2)}, u32[]{:S(2)}) collective-permute-start(bf16[1008,128]{1,0:T(8,128)(2,1)S(1)} %collective-permute-done.25.refs_6_.refs_7_), channel_id=1, source_target_pairs={{0,64},{64,128},{128,192},{192,0},{1,65},{65,129},{129,193},{193,1... | collective-permute-start | bytes 774152 | tf_op jit(solution)/shard_map/ppermute | solution.py:30
  67.9 3.9 %shard_map.121 = (bf16[2,4,192,1024]{3,2,1,0:T(8,128)(2,1)S(1)}, bf16[2,4,192,1024]{3,2,1,0:T(8,128)(2,1)S(1)}) custom-call(s32[5]{0:T(128)S(1)} %stack.74.pos._.refs_0_, bf16[4,2,2,4,24,128]{5,4,3,2,1,0:T(8,128)(2,1)S(1)} %pad_maximum_fusion.1.refs_0_, bf16[4,2,2,4,24,128]{5,4,3,2,1,0:T(8,128)(2,1)S(1)} %collective-permute-done.7.refs_1_, ...), custom_call_target="tpu_custom_call" | custom-call | bytes 6291456 | tf_op jit(solution)/shard_map/pallas_call | solution.py:67
  71.8 6.7 %collective-permute-done.26.refs_5_.refs_6_ = bf16[1008,128]{1,0:T(8,128)(2,1)S(1)} collective-permute-done((bf16[1008,128]{1,0:T(8,128)(2,1)S(1)}, bf16[1008,128]{1,0:T(8,128)(2,1)S(1)}, u32[]{:S(2)}, u32[]{:S(2)}) %collective-permute-start.26) | collective-permute-done | bytes 258080 | tf_op jit(solution)/shard_map/ppermute | solution.py:30
  78.6 2.1 %shard_map.125 = bf16[1,1008,128]{2,1,0:T(8,128)(2,1)S(1)} custom-call(s32[5]{0:T(128)S(1)} %stack.74.pos._.refs_0_, bf16[2,4,192,1024]{3,2,1,0:T(8,128)(2,1)S(1)} %get-tuple-element.11.refs_1_.refs_8_, bf16[2,4,192,1024]{3,2,1,0:T(8,128)(2,1)S(1)} %get-tuple-element.10.refs_2_.refs_1_.refs_9_, bf16[3,224,1024]{2,1,0:T(8,128)(2,1)S(1)} %copy-done.2, ...), custom_call_target="tpu_custom_call" | custom-call | flops 528482304 | bytes 9302016 | tf_op jit(solution)/shard_map/pallas_call | solution.py:67
  80.7 3.5 %collective-permute-start.27 = (bf16[504,128]{1,0:T(8,128)(2,1)S(1)}, bf16[504,128]{1,0:T(8,128)(2,1)S(1)}, u32[]{:S(2)}, u32[]{:S(2)}) collective-permute-start(bf16[504,128]{1,0:T(8,128)(2,1)S(1)} %get-tuple-element.21), channel_id=1, source_target_pairs={{0,64},{64,128},{128,192},{192,0},{1,65},{65,129},{129,193},{193,1... | collective-permute-start | bytes 387080 | tf_op jit(solution)/shard_map/ppermute | solution.py:30
  84.2 0.7 collective-permute-start.29
  84.9 3.7 %shard_map.124 = bf16[2,1008,128]{2,1,0:T(8,128)(2,1)S(1)} custom-call(s32[5]{0:T(128)S(1)} %stack.74.pos._.refs_0_, bf16[2,4,192,1024]{3,2,1,0:T(8,128)(2,1)S(1)} %get-tuple-element.11.refs_1_.refs_8_, bf16[2,4,192,1024]{3,2,1,0:T(8,128)(2,1)S(1)} %get-tuple-element.10.refs_2_.refs_1_.refs_9_, bf16[3,224,1024]{2,1,0:T(8,128)(2,1)S(1)} %copy-done.2, ...), custom_call_target="tpu_custom_call" | custom-call | flops 1056964608 | bytes 9560064 | tf_op jit(solution)/shard_map/pallas_call | solution.py:67
  88.7 2.3 %collective-permute-done.27 = bf16[504,128]{1,0:T(8,128)(2,1)S(1)} collective-permute-done((bf16[504,128]{1,0:T(8,128)(2,1)S(1)}, bf16[504,128]{1,0:T(8,128)(2,1)S(1)}, u32[]{:S(2)}, u32[]{:S(2)}) %collective-permute-start.27) | collective-permute-done | bytes 129056 | tf_op jit(solution)/shard_map/ppermute | solution.py:30
  91.0 0.7 collective-permute-done.29
  91.8 2.1 %collective-permute-start.30 = (bf16[1008,128]{1,0:T(8,128)(2,1)S(1)}, bf16[1008,128]{1,0:T(8,128)(2,1)S(1)}, u32[]{:S(2)}, u32[]{:S(2)}) collective-permute-start(bf16[1008,128]{1,0:T(8,128)(2,1)S(1)} %pad_maximum_fusion.4), channel_id=1, source_target_pairs={{0,192},{64,0},{128,64},{192,128},{1,193},{65,1},{129,65},{193,129... | collective-permute-start | bytes 774152 | tf_op jit(solution)/shard_map/ppermute | solution.py:30
  93.9 1.0 collective-permute-start.28
  94.9 2.1 %shard_map.123 = bf16[1,1008,128]{2,1,0:T(8,128)(2,1)S(1)} custom-call(s32[5]{0:T(128)S(1)} %stack.74.pos._.refs_0_, bf16[2,4,192,1024]{3,2,1,0:T(8,128)(2,1)S(1)} %get-tuple-element.11.refs_1_.refs_8_, bf16[2,4,192,1024]{3,2,1,0:T(8,128)(2,1)S(1)} %get-tuple-element.10.refs_2_.refs_1_.refs_9_, bf16[3,224,1024]{2,1,0:T(8,128)(2,1)S(1)} %copy-done.2, ...), custom_call_target="tpu_custom_call" | custom-call | flops 528482304 | bytes 9302016 | tf_op jit(solution)/shard_map/pallas_call | solution.py:67
  97.0 8.9 %collective-permute-done.30.refs_2_ = bf16[1008,128]{1,0:T(8,128)(2,1)S(1)} collective-permute-done((bf16[1008,128]{1,0:T(8,128)(2,1)S(1)}, bf16[1008,128]{1,0:T(8,128)(2,1)S(1)}, u32[]{:S(2)}, u32[]{:S(2)}) %collective-permute-start.30) | collective-permute-done | bytes 258080 | tf_op jit(solution)/shard_map/ppermute | solution.py:30
  106.0 2.5 %collective-permute-done.28.refs_1_ = bf16[1008,128]{1,0:T(8,128)(2,1)S(1)} collective-permute-done((bf16[1008,128]{1,0:T(8,128)(2,1)S(1)}, bf16[1008,128]{1,0:T(8,128)(2,1)S(1)}, u32[]{:S(2)}, u32[]{:S(2)}) %collective-permute-start.28) | collective-permute-done | bytes 258080 | tf_op jit(solution)/shard_map/ppermute | solution.py:30
  108.5 0.7 shard_map.126.refs_4_.refs_0_
  109.5 4.1 %collective-permute-start.32 = (bf16[1008,128]{1,0:T(8,128)(2,1)S(1)}, bf16[1008,128]{1,0:T(8,128)(2,1)S(1)}, u32[]{:S(2)}, u32[]{:S(2)}) collective-permute-start(bf16[1008,128]{1,0:T(8,128)(2,1)S(1)} %shard_map.126.refs_4_.refs_0_), channel_id=1, source_target_pairs={{0,192},{64,0},{128,64},{192,128},{1,193},{65,1},{129,65},{193,129... | collective-permute-start | bytes 774152 | tf_op jit(solution)/shard_map/ppermute | solution.py:30
  113.7 2.6 %shard_map.127 = bf16[2,32,1,2,24,128]{5,4,3,2,1,0:T(8,128)(2,1)S(1)} custom-call(s32[5]{0:T(128)S(1)} %stack.74.pos._.refs_0_, bf16[2,4,192,1024]{3,2,1,0:T(8,128)(2,1)S(1)} %get-tuple-element.10.refs_2_.refs_1_.refs_9_, bf16[3,224,1024]{2,1,0:T(8,128)(2,1)S(1)} %copy-done.2, bf16[3,224,1024]{2,1,0:T(8,128)(2,1)S(1)} %perturbation.1.refs_4_.refs_3_, ...), custom_call_target="tpu_custom_call" | custom-call | flops 528482304 | bytes 6414336 | tf_op jit(solution)/shard_map/pallas_call | solution.py:67
  116.4 7.3 %collective-permute-done.33.refs_5_.refs_3_ = bf16[1008,128]{1,0:T(8,128)(2,1)S(1)} collective-permute-done((bf16[1008,128]{1,0:T(8,128)(2,1)S(1)}, bf16[1008,128]{1,0:T(8,128)(2,1)S(1)}, u32[]{:S(2)}, u32[]{:S(2)}) %collective-permute-start.33) | collective-permute-done | bytes 258080 | tf_op jit(solution)/shard_map/ppermute | solution.py:30
  123.9 4.2 %collective-permute-start.36 = (bf16[504,128]{1,0:T(8,128)(2,1)S(1)}, bf16[504,128]{1,0:T(8,128)(2,1)S(1)}, u32[]{:S(2)}, u32[]{:S(2)}) collective-permute-start(bf16[504,128]{1,0:T(8,128)(2,1)S(1)} %slice.121), channel_id=1, source_target_pairs={{0,192},{64,0},{128,64},{192,128},{1,193},{65,1},{129,65},{193,129... | collective-permute-start | bytes 387080 | tf_op jit(solution)/shard_map/ppermute | solution.py:30
  128.1 4.6 %shard_map.128 = bf16[2,32,2,2,24,128]{5,4,3,2,1,0:T(8,128)(2,1)S(1)} custom-call(s32[5]{0:T(128)S(1)} %stack.74.pos._.refs_0_, bf16[2,4,192,1024]{3,2,1,0:T(8,128)(2,1)S(1)} %get-tuple-element.10.refs_2_.refs_1_.refs_9_, bf16[3,224,1024]{2,1,0:T(8,128)(2,1)S(1)} %copy-done.2, bf16[3,224,1024]{2,1,0:T(8,128)(2,1)S(1)} %perturbation.1.refs_4_.refs_3_, ...), custom_call_target="tpu_custom_call" | custom-call | flops 1056964608 | bytes 6930432 | tf_op jit(solution)/shard_map/pallas_call | solution.py:67
  132.9 2.6 %shard_map.129 = bf16[2,32,1,2,24,128]{5,4,3,2,1,0:T(8,128)(2,1)S(1)} custom-call(s32[5]{0:T(128)S(1)} %stack.74.pos._.refs_0_, bf16[2,4,192,1024]{3,2,1,0:T(8,128)(2,1)S(1)} %get-tuple-element.10.refs_2_.refs_1_.refs_9_, bf16[3,224,1024]{2,1,0:T(8,128)(2,1)S(1)} %copy-done.2, bf16[3,224,1024]{2,1,0:T(8,128)(2,1)S(1)} %perturbation.1.refs_4_.refs_3_, ...), custom_call_target="tpu_custom_call" | custom-call | flops 528482304 | bytes 6414336 | tf_op jit(solution)/shard_map/pallas_call | solution.py:67
  136.2 1.2 collective-permute-done.37
  138.0 28.3 %all_to_all.5 = bf16[32,192,128]{2,1,0:T(8,128)(2,1)} all-to-all(bf16[32,192,128]{2,1,0:T(8,128)(2,1)S(1)} %bitcast.76), channel_id=1, replica_groups=mesh['dp'=4,'zl'=2,'y'=4,'x'=4,'c'=2] {'zl','y','x'}, dimensions={0} | all-to-all | bytes 3145728 | tf_op jit(solution)/shard_map/all_to_all | solution.py:26
  166.3 1.6 reduce_sum.12
  168.0 2.8 %collective-permute-start.38 = (bf16[48,128]{1,0:T(8,128)(2,1)S(1)}, bf16[48,128]{1,0:T(8,128)(2,1)S(1)}, u32[]{:S(2)}, u32[]{:S(2)}) collective-permute-start(bf16[48,128]{1,0:T(8,128)(2,1)S(1)} %get-tuple-element.32), channel_id=1, source_target_pairs={{0,192},{64,0},{128,64},{192,128},{1,193},{65,1},{129,65},{193,129... | collective-permute-start | bytes 36872 | tf_op jit(solution)/shard_map/ppermute | solution.py:30
  170.8 4.4 %collective-permute-start.39 = (bf16[48,128]{1,0:T(8,128)(2,1)S(1)}, bf16[48,128]{1,0:T(8,128)(2,1)S(1)}, u32[]{:S(2)}, u32[]{:S(2)}) collective-permute-start(bf16[48,128]{1,0:T(8,128)(2,1)S(1)} %get-tuple-element.31), channel_id=1, source_target_pairs={{0,128},{64,192},{128,0},{192,64},{1,129},{65,193},{129,1},{193,65... | collective-permute-start | bytes 36872 | tf_op jit(solution)/shard_map/ppermute | solution.py:30
  175.2 1.9 copy-done.1
  177.1 1.3 copy-done.4
  178.4 0.9 copy-done.6
  179.4 0.9 copy-done.8
  180.3 0.9 copy-done.10
  181.3 0.9 copy-done.12
  182.2 0.9 copy-done.14
  183.2 0.9 copy-done.16
  184.1 0.9 copy-done.18
  185.0 9.5 %grads.1 = (bf16[3,224,1024]{2,1,0:T(8,128)(2,1)}, bf16[3,224,1024]{2,1,0:T(8,128)(2,1)}) custom-call(bf16[1008,128]{1,0:T(8,128)(2,1)S(1)} %copy-done.6, bf16[1008,128]{1,0:T(8,128)(2,1)S(1)} %copy-done.16, bf16[1008,128]{1,0:T(8,128)(2,1)S(1)} %copy-done.18, bf16[1008,128]{1,0:T(8,128)(2,1)S(1)} %copy-done.14, ...), custom_call_target="tpu_custom_call" | custom-call | flops 2113929216 | bytes 10420224 | tf_op jit(solution)/shard_map/grads/pallas_call | solution.py:327
  194.6 1.2 shard_map.130
  (108 shorter events, 6.3 us)
Async XLA Ops:
  0.7 0.8 copy-start.20
  1.6 0.8 copy-start.21
  3.9 25.8 %copy-start.24 = (s32[224,192]{0,1:T(8,128)S(1)}, s32[224,192]{0,1:T(8,128)}, u32[]{:S(2)}) copy-start(s32[224,192]{0,1:T(8,128)} %param.15) | copy-start | bytes 516100
  4.6 11.4 %collective-permute-start.2 = (bf16[4,24,128]{2,1,0:T(8,128)(2,1)S(1)}, bf16[4,24,128]{2,1,0:T(8,128)(2,1)S(1)}, u32[]{:S(2)}, u32[]{:S(2)}) collective-permute-start(bf16[4,24,128]{2,1,0:T(8,128)(2,1)S(1)} %get-tuple-element.27), channel_id=1, source_target_pairs={{0,64},{64,128},{128,192},{192,0},{1,65},{65,129},{129,193},{193,1... | collective-permute-start | bytes 73736 | tf_op jit(solution)/shard_map/ppermute | solution.py:30
  7.9 8.1 %collective-permute-start = (bf16[4,24,128]{2,1,0:T(8,128)(2,1)S(1)}, bf16[4,24,128]{2,1,0:T(8,128)(2,1)S(1)}, u32[]{:S(2)}, u32[]{:S(2)}) collective-permute-start(bf16[4,24,128]{2,1,0:T(8,128)(2,1)S(1)} %get-tuple-element.29), channel_id=1, source_target_pairs={{0,192},{64,0},{128,64},{192,128},{1,193},{65,1},{129,65},{193,129... | collective-permute-start | bytes 73736 | tf_op jit(solution)/shard_map/ppermute | solution.py:30
  11.0 7.7 %collective-permute-start.1 = (bf16[4,24,128]{2,1,0:T(8,128)(2,1)S(1)}, bf16[4,24,128]{2,1,0:T(8,128)(2,1)S(1)}, u32[]{:S(2)}, u32[]{:S(2)}) collective-permute-start(bf16[4,24,128]{2,1,0:T(8,128)(2,1)S(1)} %get-tuple-element.28), channel_id=1, source_target_pairs={{0,128},{64,192},{128,0},{192,64},{1,129},{65,193},{129,1},{193,65... | collective-permute-start | bytes 73736 | tf_op jit(solution)/shard_map/ppermute | solution.py:30
  18.8 4.7 %collective-permute-start.3 = (bf16[4,4,24,128]{3,2,1,0:T(8,128)(2,1)S(1)}, bf16[4,4,24,128]{3,2,1,0:T(8,128)(2,1)S(1)}, u32[]{:S(2)}, u32[]{:S(2)}) collective-permute-start(bf16[4,4,24,128]{3,2,1,0:T(8,128)(2,1)S(1)} %get-tuple-element.24), channel_id=1, source_target_pairs={{0,32},{32,0},{1,33},{33,1},{2,34},{34,2},{3,35},{35,3},{4,36},{36... | collective-permute-start | bytes 294920 | tf_op jit(solution)/shard_map/ppermute | solution.py:366
  23.5 11.2 %collective-permute-start.14 = (bf16[2,2,4,24,128]{4,3,2,1,0:T(8,128)(2,1)S(1)}, bf16[2,2,4,24,128]{4,3,2,1,0:T(8,128)(2,1)S(1)}, u32[]{:S(2)}, u32[]{:S(2)}) collective-permute-start(bf16[2,2,4,24,128]{4,3,2,1,0:T(8,128)(2,1)S(1)} %get-tuple-element.22), channel_id=1, source_target_pairs={{0,24},{8,0},{16,8},{24,16},{1,25},{9,1},{17,9},{25,17},{2,26},{10... | collective-permute-start | bytes 294920 | tf_op jit(solution)/shard_map/ppermute | solution.py:30
  24.0 11.5 %collective-permute-start.15 = (bf16[2,2,4,24,128]{4,3,2,1,0:T(8,128)(2,1)S(1)}, bf16[2,2,4,24,128]{4,3,2,1,0:T(8,128)(2,1)S(1)}, u32[]{:S(2)}, u32[]{:S(2)}) collective-permute-start(bf16[2,2,4,24,128]{4,3,2,1,0:T(8,128)(2,1)S(1)} %get-tuple-element.22), channel_id=1, source_target_pairs={{0,16},{8,24},{16,0},{24,8},{1,17},{9,25},{17,1},{25,9},{2,18},{10... | collective-permute-start | bytes 294920 | tf_op jit(solution)/shard_map/ppermute | solution.py:30
  26.6 9.8 %collective-permute-start.16 = (bf16[2,2,4,24,128]{4,3,2,1,0:T(8,128)(2,1)S(1)}, bf16[2,2,4,24,128]{4,3,2,1,0:T(8,128)(2,1)S(1)}, u32[]{:S(2)}, u32[]{:S(2)}) collective-permute-start(bf16[2,2,4,24,128]{4,3,2,1,0:T(8,128)(2,1)S(1)} %get-tuple-element.22), channel_id=1, source_target_pairs={{0,8},{8,16},{16,24},{24,0},{1,9},{9,17},{17,25},{25,1},{2,10},{10... | collective-permute-start | bytes 294920 | tf_op jit(solution)/shard_map/ppermute | solution.py:30
  29.7 37.7 %copy-start.3 = (bf16[3,224,1024]{2,1,0:T(8,128)(2,1)S(1)}, bf16[3,224,1024]{2,1,0:T(8,128)(2,1)}, u32[]{:S(2)}) copy-start(bf16[3,224,1024]{2,1,0:T(8,128)(2,1)} %refs_10_.1) | copy-start | bytes 4128772
  29.9 37.5 %copy-start.19 = (bf16[3,224,1024]{2,1,0:T(8,128)(2,1)S(1)}, bf16[3,224,1024]{2,1,0:T(8,128)(2,1)}, u32[]{:S(2)}) copy-start(bf16[3,224,1024]{2,1,0:T(8,128)(2,1)} %s_ref.2) | copy-start | bytes 4128772
  30.5 12.8 %collective-permute-start.25 = (bf16[1008,128]{1,0:T(8,128)(2,1)S(1)}, bf16[1008,128]{1,0:T(8,128)(2,1)S(1)}, u32[]{:S(2)}, u32[]{:S(2)}) collective-permute-start(bf16[1008,128]{1,0:T(8,128)(2,1)S(1)} %shard_map.122.refs_5_.refs_4_), channel_id=1, source_target_pairs={{0,64},{64,128},{128,192},{192,0},{1,65},{65,129},{129,193},{193,1... | collective-permute-start | bytes 774152 | tf_op jit(solution)/shard_map/ppermute | solution.py:30
  32.0 6.4 %collective-permute-start.4 = (bf16[2,2,4,24,128]{4,3,2,1,0:T(8,128)(2,1)S(1)}, bf16[2,2,4,24,128]{4,3,2,1,0:T(8,128)(2,1)S(1)}, u32[]{:S(2)}, u32[]{:S(2)}) collective-permute-start(bf16[2,2,4,24,128]{4,3,2,1,0:T(8,128)(2,1)S(1)} %get-tuple-element.23), channel_id=1, source_target_pairs={{0,6},{2,0},{4,2},{6,4},{1,7},{3,1},{5,3},{7,5},{8,14},{10,8},{12,... | collective-permute-start | bytes 294920 | tf_op jit(solution)/shard_map/ppermute | solution.py:30
  34.7 7.2 %collective-permute-start.5 = (bf16[2,2,4,24,128]{4,3,2,1,0:T(8,128)(2,1)S(1)}, bf16[2,2,4,24,128]{4,3,2,1,0:T(8,128)(2,1)S(1)}, u32[]{:S(2)}, u32[]{:S(2)}) collective-permute-start(bf16[2,2,4,24,128]{4,3,2,1,0:T(8,128)(2,1)S(1)} %get-tuple-element.23), channel_id=1, source_target_pairs={{0,4},{2,6},{4,0},{6,2},{1,5},{3,7},{5,1},{7,3},{8,12},{10,14},{12... | collective-permute-start | bytes 294920 | tf_op jit(solution)/shard_map/ppermute | solution.py:30
  35.5 7.6 %collective-permute-start.6 = (bf16[2,2,4,24,128]{4,3,2,1,0:T(8,128)(2,1)S(1)}, bf16[2,2,4,24,128]{4,3,2,1,0:T(8,128)(2,1)S(1)}, u32[]{:S(2)}, u32[]{:S(2)}) collective-permute-start(bf16[2,2,4,24,128]{4,3,2,1,0:T(8,128)(2,1)S(1)} %get-tuple-element.23), channel_id=1, source_target_pairs={{0,2},{2,4},{4,6},{6,0},{1,3},{3,5},{5,7},{7,1},{8,10},{10,12},{12... | collective-permute-start | bytes 294920 | tf_op jit(solution)/shard_map/ppermute | solution.py:30
  36.5 10.8 %collective-permute-start.18 = (bf16[4,2,2,4,24,128]{5,4,3,2,1,0:T(8,128)(2,1)S(1)}, bf16[4,2,2,4,24,128]{5,4,3,2,1,0:T(8,128)(2,1)S(1)}, u32[]{:S(2)}, u32[]{:S(2)}) collective-permute-start(bf16[4,2,2,4,24,128]{5,4,3,2,1,0:T(8,128)(2,1)S(1)} %pad_maximum_fusion.2.refs_8_), channel_id=1, source_target_pairs={{0,2},{2,4},{4,6},{6,0},{1,3},{3,5},{5,7},{7,1},{8,10},{10,12},{12... | collective-permute-start | bytes 1179656 | tf_op jit(solution)/shard_map/ppermute | solution.py:30
  38.4 9.0 %collective-permute-start.17 = (bf16[4,2,2,4,24,128]{5,4,3,2,1,0:T(8,128)(2,1)S(1)}, bf16[4,2,2,4,24,128]{5,4,3,2,1,0:T(8,128)(2,1)S(1)}, u32[]{:S(2)}, u32[]{:S(2)}) collective-permute-start(bf16[4,2,2,4,24,128]{5,4,3,2,1,0:T(8,128)(2,1)S(1)} %pad_maximum_fusion.2.refs_8_), channel_id=1, source_target_pairs={{0,6},{2,0},{4,2},{6,4},{1,7},{3,1},{5,3},{7,5},{8,14},{10,8},{12,... | collective-permute-start | bytes 1179656 | tf_op jit(solution)/shard_map/ppermute | solution.py:30
  41.9 5.4 %collective-permute-start.20 = (bf16[4,2,2,4,24,128]{5,4,3,2,1,0:T(8,128)(2,1)S(1)}, bf16[4,2,2,4,24,128]{5,4,3,2,1,0:T(8,128)(2,1)S(1)}, u32[]{:S(2)}, u32[]{:S(2)}) collective-permute-start(bf16[4,2,2,4,24,128]{5,4,3,2,1,0:T(8,128)(2,1)S(1)} %pad_maximum_fusion.2.refs_8_), channel_id=1, source_target_pairs={{0,1},{1,0},{2,3},{3,2},{4,5},{5,4},{6,7},{7,6},{8,9},{9,8},{10,11... | collective-permute-start | bytes 1179656 | tf_op jit(solution)/shard_map/ppermute | solution.py:184
  43.2 10.4 %collective-permute-start.8 = (bf16[4,2,2,4,24,128]{5,4,3,2,1,0:T(8,128)(2,1)S(1)}, bf16[4,2,2,4,24,128]{5,4,3,2,1,0:T(8,128)(2,1)S(1)}, u32[]{:S(2)}, u32[]{:S(2)}) collective-permute-start(bf16[4,2,2,4,24,128]{5,4,3,2,1,0:T(8,128)(2,1)S(1)} %pad_maximum_fusion.1.refs_0_), channel_id=1, source_target_pairs={{0,8},{8,16},{16,24},{24,0},{1,9},{9,17},{17,25},{25,1},{2,10},{10... | collective-permute-start | bytes 1179656 | tf_op jit(solution)/shard_map/ppermute | solution.py:30
  43.3 84.7 %copy-start.7 = (bf16[1008,128]{1,0:T(8,128)(2,1)}, bf16[1008,128]{1,0:T(8,128)(2,1)S(1)}, u32[]{:S(2)}) copy-start(bf16[1008,128]{1,0:T(8,128)(2,1)S(1)} %collective-permute-done.25.refs_6_.refs_7_) | copy-start | bytes 774148
  43.3 10.5 %collective-permute-start.7 = (bf16[4,2,2,4,24,128]{5,4,3,2,1,0:T(8,128)(2,1)S(1)}, bf16[4,2,2,4,24,128]{5,4,3,2,1,0:T(8,128)(2,1)S(1)}, u32[]{:S(2)}, u32[]{:S(2)}) collective-permute-start(bf16[4,2,2,4,24,128]{5,4,3,2,1,0:T(8,128)(2,1)S(1)} %pad_maximum_fusion.1.refs_0_), channel_id=1, source_target_pairs={{0,24},{8,0},{16,8},{24,16},{1,25},{9,1},{17,9},{25,17},{2,26},{10... | collective-permute-start | bytes 1179656 | tf_op jit(solution)/shard_map/ppermute | solution.py:30
  47.3 6.5 %collective-permute-start.10 = (bf16[4,2,2,4,24,128]{5,4,3,2,1,0:T(8,128)(2,1)S(1)}, bf16[4,2,2,4,24,128]{5,4,3,2,1,0:T(8,128)(2,1)S(1)}, u32[]{:S(2)}, u32[]{:S(2)}) collective-permute-start(bf16[4,2,2,4,24,128]{5,4,3,2,1,0:T(8,128)(2,1)S(1)} %pad_maximum_fusion.1.refs_0_), channel_id=1, source_target_pairs={{0,1},{1,0},{2,3},{3,2},{4,5},{5,4},{6,7},{7,6},{8,9},{9,8},{10,11... | collective-permute-start | bytes 1179656 | tf_op jit(solution)/shard_map/ppermute | solution.py:184
  47.3 12.7 %collective-permute-start.19 = (bf16[4,2,2,4,24,128]{5,4,3,2,1,0:T(8,128)(2,1)S(1)}, bf16[4,2,2,4,24,128]{5,4,3,2,1,0:T(8,128)(2,1)S(1)}, u32[]{:S(2)}, u32[]{:S(2)}) collective-permute-start(bf16[4,2,2,4,24,128]{5,4,3,2,1,0:T(8,128)(2,1)S(1)} %collective-permute-done.18.refs_11_), channel_id=1, source_target_pairs={{0,2},{2,4},{4,6},{6,0},{1,3},{3,5},{5,7},{7,1},{8,10},{10,12},{12... | collective-permute-start | bytes 1179656 | tf_op jit(solution)/shard_map/ppermute | solution.py:30
  47.3 12.7 %collective-permute-start.21 = (bf16[4,2,2,4,24,128]{5,4,3,2,1,0:T(8,128)(2,1)S(1)}, bf16[4,2,2,4,24,128]{5,4,3,2,1,0:T(8,128)(2,1)S(1)}, u32[]{:S(2)}, u32[]{:S(2)}) collective-permute-start(bf16[4,2,2,4,24,128]{5,4,3,2,1,0:T(8,128)(2,1)S(1)} %collective-permute-done.17.refs_9_), channel_id=1, source_target_pairs={{0,1},{1,0},{2,3},{3,2},{4,5},{5,4},{6,7},{7,6},{8,9},{9,8},{10,11... | collective-permute-start | bytes 1179656 | tf_op jit(solution)/shard_map/ppermute | solution.py:184
  53.6 9.5 %collective-permute-start.9 = (bf16[4,2,2,4,24,128]{5,4,3,2,1,0:T(8,128)(2,1)S(1)}, bf16[4,2,2,4,24,128]{5,4,3,2,1,0:T(8,128)(2,1)S(1)}, u32[]{:S(2)}, u32[]{:S(2)}) collective-permute-start(bf16[4,2,2,4,24,128]{5,4,3,2,1,0:T(8,128)(2,1)S(1)} %collective-permute-done.8.refs_3_), channel_id=1, source_target_pairs={{0,8},{8,16},{16,24},{24,0},{1,9},{9,17},{17,25},{25,1},{2,10},{10... | collective-permute-start | bytes 1179656 | tf_op jit(solution)/shard_map/ppermute | solution.py:30
  53.9 9.2 %collective-permute-start.23 = (bf16[4,2,2,4,24,128]{5,4,3,2,1,0:T(8,128)(2,1)S(1)}, bf16[4,2,2,4,24,128]{5,4,3,2,1,0:T(8,128)(2,1)S(1)}, u32[]{:S(2)}, u32[]{:S(2)}) collective-permute-start(bf16[4,2,2,4,24,128]{5,4,3,2,1,0:T(8,128)(2,1)S(1)} %collective-permute-done.18.refs_11_), channel_id=1, source_target_pairs={{0,1},{1,0},{2,3},{3,2},{4,5},{5,4},{6,7},{7,6},{8,9},{9,8},{10,11... | collective-permute-start | bytes 1179656 | tf_op jit(solution)/shard_map/ppermute | solution.py:184
  53.9 14.0 %collective-permute-start.13 = (bf16[4,2,2,4,24,128]{5,4,3,2,1,0:T(8,128)(2,1)S(1)}, bf16[4,2,2,4,24,128]{5,4,3,2,1,0:T(8,128)(2,1)S(1)}, u32[]{:S(2)}, u32[]{:S(2)}) collective-permute-start(bf16[4,2,2,4,24,128]{5,4,3,2,1,0:T(8,128)(2,1)S(1)} %collective-permute-done.8.refs_3_), channel_id=1, source_target_pairs={{0,1},{1,0},{2,3},{3,2},{4,5},{5,4},{6,7},{7,6},{8,9},{9,8},{10,11... | collective-permute-start | bytes 1179656 | tf_op jit(solution)/shard_map/ppermute | solution.py:184
  60.1 7.7 %collective-permute-start.11 = (bf16[4,2,2,4,24,128]{5,4,3,2,1,0:T(8,128)(2,1)S(1)}, bf16[4,2,2,4,24,128]{5,4,3,2,1,0:T(8,128)(2,1)S(1)}, u32[]{:S(2)}, u32[]{:S(2)}) collective-permute-start(bf16[4,2,2,4,24,128]{5,4,3,2,1,0:T(8,128)(2,1)S(1)} %collective-permute-done.7.refs_1_), channel_id=1, source_target_pairs={{0,1},{1,0},{2,3},{3,2},{4,5},{5,4},{6,7},{7,6},{8,9},{9,8},{10,11... | collective-permute-start | bytes 1179656 | tf_op jit(solution)/shard_map/ppermute | solution.py:184
  60.1 7.8 %collective-permute-start.22 = (bf16[4,2,2,4,24,128]{5,4,3,2,1,0:T(8,128)(2,1)S(1)}, bf16[4,2,2,4,24,128]{5,4,3,2,1,0:T(8,128)(2,1)S(1)}, u32[]{:S(2)}, u32[]{:S(2)}) collective-permute-start(bf16[4,2,2,4,24,128]{5,4,3,2,1,0:T(8,128)(2,1)S(1)} %collective-permute-done.19.refs_10_), channel_id=1, source_target_pairs={{0,1},{1,0},{2,3},{3,2},{4,5},{5,4},{6,7},{7,6},{8,9},{9,8},{10,11... | collective-permute-start | bytes 1179656 | tf_op jit(solution)/shard_map/ppermute | solution.py:184
  63.0 4.9 %collective-permute-start.12 = (bf16[4,2,2,4,24,128]{5,4,3,2,1,0:T(8,128)(2,1)S(1)}, bf16[4,2,2,4,24,128]{5,4,3,2,1,0:T(8,128)(2,1)S(1)}, u32[]{:S(2)}, u32[]{:S(2)}) collective-permute-start(bf16[4,2,2,4,24,128]{5,4,3,2,1,0:T(8,128)(2,1)S(1)} %collective-permute-done.9.refs_2_), channel_id=1, source_target_pairs={{0,1},{1,0},{2,3},{3,2},{4,5},{5,4},{6,7},{7,6},{8,9},{9,8},{10,11... | collective-permute-start | bytes 1179656 | tf_op jit(solution)/shard_map/ppermute | solution.py:184
  63.0 15.5 %collective-permute-start.26 = (bf16[1008,128]{1,0:T(8,128)(2,1)S(1)}, bf16[1008,128]{1,0:T(8,128)(2,1)S(1)}, u32[]{:S(2)}, u32[]{:S(2)}) collective-permute-start(bf16[1008,128]{1,0:T(8,128)(2,1)S(1)} %collective-permute-done.25.refs_6_.refs_7_), channel_id=1, source_target_pairs={{0,64},{64,128},{128,192},{192,0},{1,65},{65,129},{129,193},{193,1... | collective-permute-start | bytes 774152 | tf_op jit(solution)/shard_map/ppermute | solution.py:30
  67.8 10.8 %copy-start.2 = (bf16[3,224,1024]{2,1,0:T(8,128)(2,1)S(1)}, bf16[3,224,1024]{2,1,0:T(8,128)(2,1)}, u32[]{:S(2)}) copy-start(bf16[3,224,1024]{2,1,0:T(8,128)(2,1)} %refs_2_.5) | copy-start | bytes 4128772
  67.8 17.1 %collective-permute-start.24 = (bf16[1008,128]{1,0:T(8,128)(2,1)S(1)}, bf16[1008,128]{1,0:T(8,128)(2,1)S(1)}, u32[]{:S(2)}, u32[]{:S(2)}) collective-permute-start(bf16[1008,128]{1,0:T(8,128)(2,1)S(1)} %shard_map.122.refs_5_.refs_4_), channel_id=1, source_target_pairs={{0,192},{64,0},{128,64},{192,128},{1,193},{65,1},{129,65},{193,129... | collective-permute-start | bytes 774152 | tf_op jit(solution)/shard_map/ppermute | solution.py:30
  71.8 23.1 %copy-start = (bf16[2,4,192,1024]{3,2,1,0:T(8,128)(2,1)}, bf16[2,4,192,1024]{3,2,1,0:T(8,128)(2,1)S(1)}, u32[]{:S(2)}) copy-start(bf16[2,4,192,1024]{3,2,1,0:T(8,128)(2,1)S(1)} %get-tuple-element.11.refs_1_.refs_8_) | copy-start | bytes 9437188
  78.6 54.3 %copy-start.11 = (bf16[1008,128]{1,0:T(8,128)(2,1)}, bf16[1008,128]{1,0:T(8,128)(2,1)S(1)}, u32[]{:S(2)}) copy-start(bf16[1008,128]{1,0:T(8,128)(2,1)S(1)} %collective-permute-done.26.refs_5_.refs_6_) | copy-start | bytes 774148
  80.7 10.2 %collective-permute-start.27 = (bf16[504,128]{1,0:T(8,128)(2,1)S(1)}, bf16[504,128]{1,0:T(8,128)(2,1)S(1)}, u32[]{:S(2)}, u32[]{:S(2)}) collective-permute-start(bf16[504,128]{1,0:T(8,128)(2,1)S(1)} %get-tuple-element.21), channel_id=1, source_target_pairs={{0,64},{64,128},{128,192},{192,0},{1,65},{65,129},{129,193},{193,1... | collective-permute-start | bytes 387080 | tf_op jit(solution)/shard_map/ppermute | solution.py:30
  84.2 7.5 %collective-permute-start.29 = (bf16[504,128]{1,0:T(8,128)(2,1)S(1)}, bf16[504,128]{1,0:T(8,128)(2,1)S(1)}, u32[]{:S(2)}, u32[]{:S(2)}) collective-permute-start(bf16[504,128]{1,0:T(8,128)(2,1)S(1)} %get-tuple-element.20), channel_id=1, source_target_pairs={{0,192},{64,0},{128,64},{192,128},{1,193},{65,1},{129,65},{193,129... | collective-permute-start | bytes 387080 | tf_op jit(solution)/shard_map/ppermute | solution.py:30
  84.9 43.1 %copy-start.9 = (bf16[1008,128]{1,0:T(8,128)(2,1)}, bf16[1008,128]{1,0:T(8,128)(2,1)S(1)}, u32[]{:S(2)}) copy-start(bf16[1008,128]{1,0:T(8,128)(2,1)S(1)} %collective-permute-done.24.refs_5_.refs_6_) | copy-start | bytes 774148
  91.8 14.2 %collective-permute-start.30 = (bf16[1008,128]{1,0:T(8,128)(2,1)S(1)}, bf16[1008,128]{1,0:T(8,128)(2,1)S(1)}, u32[]{:S(2)}, u32[]{:S(2)}) collective-permute-start(bf16[1008,128]{1,0:T(8,128)(2,1)S(1)} %pad_maximum_fusion.4), channel_id=1, source_target_pairs={{0,192},{64,0},{128,64},{192,128},{1,193},{65,1},{129,65},{193,129... | collective-permute-start | bytes 774152 | tf_op jit(solution)/shard_map/ppermute | solution.py:30
  93.9 14.6 %collective-permute-start.28 = (bf16[1008,128]{1,0:T(8,128)(2,1)S(1)}, bf16[1008,128]{1,0:T(8,128)(2,1)S(1)}, u32[]{:S(2)}, u32[]{:S(2)}) collective-permute-start(bf16[1008,128]{1,0:T(8,128)(2,1)S(1)} %pad_maximum_fusion.3), channel_id=1, source_target_pairs={{0,64},{64,128},{128,192},{192,0},{1,65},{65,129},{129,193},{193,1... | collective-permute-start | bytes 774152 | tf_op jit(solution)/shard_map/ppermute | solution.py:30
  109.2 7.0 %copy-start.5 = (bf16[1008,128]{1,0:T(8,128)(2,1)}, bf16[1008,128]{1,0:T(8,128)(2,1)S(1)}, u32[]{:S(2)}) copy-start(bf16[1008,128]{1,0:T(8,128)(2,1)S(1)} %shard_map.126.refs_4_.refs_0_) | copy-start | bytes 774148
  109.2 14.5 %collective-permute-start.33 = (bf16[1008,128]{1,0:T(8,128)(2,1)S(1)}, bf16[1008,128]{1,0:T(8,128)(2,1)S(1)}, u32[]{:S(2)}, u32[]{:S(2)}) collective-permute-start(bf16[1008,128]{1,0:T(8,128)(2,1)S(1)} %shard_map.126.refs_4_.refs_0_), channel_id=1, source_target_pairs={{0,64},{64,128},{128,192},{192,0},{1,65},{65,129},{129,193},{193,1... | collective-permute-start | bytes 774152 | tf_op jit(solution)/shard_map/ppermute | solution.py:30
  109.5 14.3 %collective-permute-start.32 = (bf16[1008,128]{1,0:T(8,128)(2,1)S(1)}, bf16[1008,128]{1,0:T(8,128)(2,1)S(1)}, u32[]{:S(2)}, u32[]{:S(2)}) collective-permute-start(bf16[1008,128]{1,0:T(8,128)(2,1)S(1)} %shard_map.126.refs_4_.refs_0_), channel_id=1, source_target_pairs={{0,192},{64,0},{128,64},{192,128},{1,193},{65,1},{129,65},{193,129... | collective-permute-start | bytes 774152 | tf_op jit(solution)/shard_map/ppermute | solution.py:30
  116.3 19.8 %collective-permute-start.31 = (bf16[32,1,2,24,128]{4,3,2,1,0:T(8,128)(2,1)S(1)}, bf16[32,1,2,24,128]{4,3,2,1,0:T(8,128)(2,1)S(1)}, u32[]{:S(2)}, u32[]{:S(2)}) collective-permute-start(bf16[32,1,2,24,128]{4,3,2,1,0:T(8,128)(2,1)S(1)} %slice_bitcast_fusion.4), channel_id=1, source_target_pairs={{0,1},{1,0},{2,3},{3,2},{4,5},{5,4},{6,7},{7,6},{8,9},{9,8},{10,11... | collective-permute-start | bytes 1179656 | tf_op jit(solution)/shard_map/ppermute | solution.py:343
  123.7 8.9 %copy-start.13 = (bf16[1008,128]{1,0:T(8,128)(2,1)}, bf16[1008,128]{1,0:T(8,128)(2,1)S(1)}, u32[]{:S(2)}) copy-start(bf16[1008,128]{1,0:T(8,128)(2,1)S(1)} %collective-permute-done.33.refs_5_.refs_3_) | copy-start | bytes 774148
  123.8 9.1 %collective-permute-start.35 = (bf16[504,128]{1,0:T(8,128)(2,1)S(1)}, bf16[504,128]{1,0:T(8,128)(2,1)S(1)}, u32[]{:S(2)}, u32[]{:S(2)}) collective-permute-start(bf16[504,128]{1,0:T(8,128)(2,1)S(1)} %slice.120), channel_id=1, source_target_pairs={{0,64},{64,128},{128,192},{192,0},{1,65},{65,129},{129,193},{193,1... | collective-permute-start | bytes 387080 | tf_op jit(solution)/shard_map/ppermute | solution.py:30
  123.9 8.8 %copy-start.15 = (bf16[1008,128]{1,0:T(8,128)(2,1)}, bf16[1008,128]{1,0:T(8,128)(2,1)S(1)}, u32[]{:S(2)}) copy-start(bf16[1008,128]{1,0:T(8,128)(2,1)S(1)} %collective-permute-done.32.refs_4_.refs_1_) | copy-start | bytes 774148
  123.9 9.0 %collective-permute-start.36 = (bf16[504,128]{1,0:T(8,128)(2,1)S(1)}, bf16[504,128]{1,0:T(8,128)(2,1)S(1)}, u32[]{:S(2)}, u32[]{:S(2)}) collective-permute-start(bf16[504,128]{1,0:T(8,128)(2,1)S(1)} %slice.121), channel_id=1, source_target_pairs={{0,192},{64,0},{128,64},{192,128},{1,193},{65,1},{129,65},{193,129... | collective-permute-start | bytes 387080 | tf_op jit(solution)/shard_map/ppermute | solution.py:30
  132.7 4.9 %collective-permute-start.34 = (bf16[32,2,2,24,128]{4,3,2,1,0:T(8,128)(2,1)S(1)}, bf16[32,2,2,24,128]{4,3,2,1,0:T(8,128)(2,1)S(1)}, u32[]{:S(2)}, u32[]{:S(2)}) collective-permute-start(bf16[32,2,2,24,128]{4,3,2,1,0:T(8,128)(2,1)S(1)} %slice_bitcast_fusion), channel_id=1, source_target_pairs={{0,1},{1,0},{2,3},{3,2},{4,5},{5,4},{6,7},{7,6},{8,9},{9,8},{10,11... | collective-permute-start | bytes 2359304 | tf_op jit(solution)/shard_map/ppermute | solution.py:343
  132.9 2.6 %copy-start.17 = (bf16[1008,128]{1,0:T(8,128)(2,1)}, bf16[1008,128]{1,0:T(8,128)(2,1)S(1)}, u32[]{:S(2)}) copy-start(bf16[1008,128]{1,0:T(8,128)(2,1)S(1)} %constant_dynamic-update-slice_fusion.refs_4_.refs_2_) | copy-start | bytes 774148
  135.6 1.9 collective-permute-start.37
  168.0 26.6 %collective-permute-start.38 = (bf16[48,128]{1,0:T(8,128)(2,1)S(1)}, bf16[48,128]{1,0:T(8,128)(2,1)S(1)}, u32[]{:S(2)}, u32[]{:S(2)}) collective-permute-start(bf16[48,128]{1,0:T(8,128)(2,1)S(1)} %get-tuple-element.32), channel_id=1, source_target_pairs={{0,192},{64,0},{128,64},{192,128},{1,193},{65,1},{129,65},{193,129... | collective-permute-start | bytes 36872 | tf_op jit(solution)/shard_map/ppermute | solution.py:30
  170.8 23.8 %collective-permute-start.39 = (bf16[48,128]{1,0:T(8,128)(2,1)S(1)}, bf16[48,128]{1,0:T(8,128)(2,1)S(1)}, u32[]{:S(2)}, u32[]{:S(2)}) collective-permute-start(bf16[48,128]{1,0:T(8,128)(2,1)S(1)} %get-tuple-element.31), channel_id=1, source_target_pairs={{0,128},{64,192},{128,0},{192,64},{1,129},{65,193},{129,1},{193,65... | collective-permute-start | bytes 36872 | tf_op jit(solution)/shard_map/ppermute | solution.py:30
  175.2 19.4 %collective-permute-start.40 = (bf16[48,128]{1,0:T(8,128)(2,1)S(1)}, bf16[48,128]{1,0:T(8,128)(2,1)S(1)}, u32[]{:S(2)}, u32[]{:S(2)}) collective-permute-start(bf16[48,128]{1,0:T(8,128)(2,1)S(1)} %get-tuple-element.30), channel_id=1, source_target_pairs={{0,64},{64,128},{128,192},{192,0},{1,65},{65,129},{129,193},{193,1... | collective-permute-start | bytes 36872 | tf_op jit(solution)/shard_map/ppermute | solution.py:30
  175.2 1.9 copy-start.1
  177.1 1.3 copy-start.4
  178.4 0.9 copy-start.6
  179.4 0.9 copy-start.8
  180.3 0.9 copy-start.10
  181.3 0.9 copy-start.12
  182.2 0.9 copy-start.14
  183.2 0.9 copy-start.16
  184.1 0.9 copy-start.18
  (2 other events, 1.5 us)
